TPU v7x, 32 devices: a whole 2x2x4 slice. The times are simulated.
32 devices in a mesh: dom: 4 (over x, core), sub: 8 (over z, y).
Axes of the slice: x: 2, y: 2, z: 4, core: 2. Of those that a mesh axis runs over, the one named last changes fastest.
Arguments:
- feats: bfloat16 [65536, 256], P(('dom', 'sub')), may hold values from -6 to 6
- w_self: bfloat16 [256, 256], replicated, may hold values from -0.375 to 0.375
- w_neigh: bfloat16 [256, 256], replicated, may hold values from -0.375 to 0.375
- cotangent: bfloat16 [65536, 256], P(('dom', 'sub')), may hold values from -6 to 6
- hub_rows: int32 [1024], P(('dom', 'sub')), may hold values from 0 to 2047
- send_rows: int32 [16384], P(('dom', 'sub')), may hold values from 0 to 2047
- edge_src: int32 [2097152], P(('dom', 'sub')), may hold values from 0 to 3583
- edge_dst: int32 [2097152], P(('dom', 'sub')), may hold values from 0 to 2047
Outputs:
- layer_out: bfloat16 [65536, 256], P(('dom', 'sub'))
- grad_feats: bfloat16 [65536, 256], P(('dom', 'sub'))
- grad_self: float32 [256, 256], replicated
- grad_neigh: float32 [256, 256], replicated
All inputs are finite; a program needn't handle non-finite values.
Results may differ from a plain program's by a relative error of at most 0.0051.
Values may be sent and summed in bfloat16 or wider, within the bound.
No kernel may reach another device: no remote copies, remote signals or barrier semaphores. Data moves between devices by JAX's collectives and lax.ppermute only.
A program may use at most 320 MiB of HBM per device.

v0:
```python
import jax
import jax.numpy as jnp
from jax import lax
from jax.sharding import PartitionSpec as P


def silu_parts(pre):
    sig = jax.nn.sigmoid(pre)
    return (pre * sig, sig * (1.0 + pre * (1.0 - sig)))


def body(feats, w_self, w_neigh, cotangent, hub_rows, send_rows, edge_src, edge_dst):
    vcount = feats.shape[0]
    hubs = lax.all_gather(feats[hub_rows], ("dom", "sub"), axis=0, tiled=True)
    outgoing = feats[send_rows]
    received = lax.all_to_all(outgoing, ("dom", "sub"), split_axis=0, concat_axis=0, tiled=True)
    table = jnp.concatenate([feats, hubs, received], axis=0)
    slot_count = table.shape[0]
    flat_index = edge_dst * slot_count + edge_src
    counts = (
        jnp.zeros((vcount * slot_count,), jnp.float32)
        .at[flat_index]
        .add(1.0)
        .reshape(vcount, slot_count)
    )
    degree = jnp.sum(counts, axis=1)
    inverse = 1.0 / jnp.maximum(degree, 1.0)
    adjacency = counts.astype(jnp.bfloat16)
    total = jnp.dot(adjacency, table, preferred_element_type=jnp.float32)
    mean = (total * inverse[:, None]).astype(jnp.bfloat16)
    pre = jnp.dot(feats, w_self, preferred_element_type=jnp.float32) + jnp.dot(
        mean, w_neigh, preferred_element_type=jnp.float32
    )
    act, slope = silu_parts(pre)
    layer_out = act.astype(jnp.bfloat16)
    grad_pre = (cotangent.astype(jnp.float32) * slope).astype(jnp.bfloat16)
    part_self = jnp.dot(feats.T, grad_pre, preferred_element_type=jnp.float32)
    part_neigh = jnp.dot(mean.T, grad_pre, preferred_element_type=jnp.float32)
    grad_self, grad_neigh = lax.psum((part_self, part_neigh), ("dom", "sub"))
    dmsg = (
        jnp.dot(grad_pre, w_neigh.T, preferred_element_type=jnp.float32) * inverse[:, None]
    ).astype(jnp.bfloat16)
    hub_total = hubs.shape[0]
    slot = lax.dot_general(
        adjacency, dmsg, (((0,), (0,)), ((), ())), preferred_element_type=jnp.float32
    )
    local = slot[:vcount]
    hub_part = slot[vcount : vcount + hub_total]
    halo_part = slot[vcount + hub_total :]
    hub_whole = lax.psum(hub_part, ("dom", "sub"))
    hub_back = lax.dynamic_slice_in_dim(
        hub_whole, lax.axis_index(("dom", "sub")) * hub_rows.shape[0], hub_rows.shape[0], 0
    )
    returned = lax.all_to_all(
        halo_part.astype(jnp.bfloat16), ("dom", "sub"), split_axis=0, concat_axis=0, tiled=True
    ).astype(halo_part.dtype)
    grad_feats = jnp.dot(grad_pre, w_self.T, preferred_element_type=jnp.float32) + local
    grad_feats = grad_feats + jax.ops.segment_sum(hub_back, hub_rows, num_segments=vcount)
    grad_feats = grad_feats + jax.ops.segment_sum(returned, send_rows, num_segments=vcount)
    return (layer_out, grad_feats.astype(jnp.bfloat16), grad_self, grad_neigh)


def solution(mesh):
    return jax.shard_map(
        body,
        mesh=mesh,
        in_specs=(
            P(("dom", "sub"), None),
            P(),
            P(),
            P(("dom", "sub"), None),
            P(("dom", "sub")),
            P(("dom", "sub")),
            P(("dom", "sub")),
            P(("dom", "sub")),
        ),
        out_specs=(P(("dom", "sub"), None), P(("dom", "sub"), None), P(), P()),
        check_vma=False,
    )
```

profile of v0, /device:TPU:0, one launch (start us, length us, event | category | flops | bytes accessed | tf_op | source)
XLA Modules:
  0.0 672.6 jit_solution(16232055544795427992)
XLA Ops:
  7.2 0.0 copy-start
  7.2 0.0 copy-start.3
  7.2 0.0 copy-start.4
  7.2 0.7 compare_select_fusion.1
  8.0 3.6 gather_fusion.1
  11.5 7.3 %all-to-all-start = ((bf16[32,16,256]{2,1,0:T(8,128)(2,1)}), bf16[32,16,256]{2,1,0:T(8,128)(2,1)S(1)}, u32[]{:S(2)}, u32[]{:S(2)}) async-start(bf16[32,16,256]{2,1,0:T(8,128)(2,1)} %bitcast), calls=%async_computation | async-start | bytes 524288 | tf_op jit(solution)/shard_map/all_to_all | solution.py:16
  18.8 0.0 all-reduce.3.cloned.1.call-start
  18.9 0.0 copy-done.3
  18.9 0.0 copy-done.4
  19.0 352.9 %scatter_custom_fusion = f32[7340032]{0:T(1024)} fusion(s32[65536]{0:T(1024)S(1)} %compare_select_fusion, f32[65536]{0:T(1024)S(1)} %broadcast.17, f32[]{:T(128)} %constant.11.clone.1), kind=kCustom, calls=%fused_computation.4 | custom fusion | flops 65536 | bytes 29360132 | tf_op jit(solution)/shard_map/scatter-add | solution.py:23
  371.8 30.4 %reshape.21 = f32[2048,3584]{1,0:T(8,128)} reshape(f32[7340032]{0:T(1024)} %scatter_custom_fusion) | data formatting | bytes 58720256 | tf_op jit(solution)/shard_map/reshape | solution.py:24
  402.3 0.0 copy-start.8
  402.3 0.0 copy-start.1
  402.3 0.0 copy-start.2
  402.3 11.1 %reduce_sum.9 = f32[2048]{0:T(1024)S(1)} reduce(f32[2048,3584]{1,0:T(8,128)} %reshape.21, f32[]{:T(128)} %constant.11.clone.1), dimensions={1}, to_apply=%region_1.0 | reduce | flops 7337984 | bytes 29368324 | tf_op jit(solution)/shard_map/reduce_sum | solution.py:26
  413.4 0.0 copy-done.8
  413.5 0.0 copy-done.1
  413.5 0.6 gather_fusion
  414.1 71.9 %all-gather = bf16[1024,256]{1,0:T(8,128)(2,1)S(1)} all-gather(bf16[32,256]{1,0:T(8,128)(2,1)S(1)} %gather_fusion), channel_id=2, replica_groups=mesh['dom'=4,'sub'=8] {'dom','sub'}, dimensions={0}, use_global_device_ids=true | all-gather | bytes 540672 | tf_op jit(solution)/shard_map/all_gather | solution.py:14
  486.0 0.0 copy-done.2
  486.0 1.8 fusion.24
  487.8 0.0 all-to-all-done
  487.8 13.4 %fusion.9 = bf16[2048,256]{1,0:T(8,128)(2,1)S(1)} fusion(f32[2048,3584]{1,0:T(8,128)} %reshape.21, bf16[512,256]{1,0:T(8,128)(2,1)S(1)} %bitcast.22, bf16[1024,256]{1,0:T(8,128)(2,1)S(1)} %all-gather, bf16[2048,256]{1,0:T(8,128)(2,1)S(1)} %copy-done.1, f32[2048]{0:T(1024)S(1)} %maximum_divide_fusion), kind=kOutput, calls=%fused_computation.14 | convolution fusion | flops 3771990016 | bytes 32251904 | tf_op jit(solution)/shard_map/dot_general | solution.py:29
  501.2 0.0 copy-done
  501.2 4.1 multiply_convert_fusion
  505.3 14.1 %fusion.2 = f32[3584,256]{1,0:T(8,128)} fusion(f32[2048,3584]{1,0:T(8,128)} %reshape.21, bf16[2048,256]{1,0:T(8,128)(2,1)S(1)} %get-tuple-element.19, bf16[256,256]{1,0:T(8,128)(2,1)S(1)} %copy-done, f32[2048]{0:T(1024)S(1)} %maximum_divide_fusion), kind=kOutput, calls=%fused_computation.6 | convolution fusion | flops 4034920448 | bytes 34217984 | tf_op jit(solution)/shard_map/dot_general | solution.py:44
  519.4 1.2 fusion.25
  520.5 1.2 convolution_bitcast_fusion
  521.7 0.0 copy-start.7
  521.7 2.3 slice.18
  524.0 0.0 all-reduce.3.cloned.1.call-update
  524.0 1.8 slice.22
  525.8 2.6 all-to-all-start.1
  528.4 0.0 copy-done.7
  528.4 0.1 add_reduce_fusion
  528.5 2.1 convolution_add_fusion
  530.6 10.6 %all-to-all-done.1 = bf16[32,16,256]{2,1,0:T(8,128)(2,1)S(1)} async-done(((bf16[32,16,256]{2,1,0:T(8,128)(2,1)}), bf16[32,16,256]{2,1,0:T(8,128)(2,1)S(1)}, u32[]{:S(2)}, u32[]{:S(2)}) %all-to-all-start.1) | async-done | bytes 262176 | tf_op jit(solution)/shard_map/all_to_all | solution.py:54
  541.3 0.1 bitcast_convert_fusion
  541.3 114.3 %all-reduce.3.cloned.1.call-done = (f32[1024,256]{1,0:T(8,128)}, f32[256,256]{0,1:T(8,128)}, f32[256,256]{1,0:T(8,128)}) async-done(((f32[1024,256]{1,0:T(8,128)}, f32[256,256]{0,1:T(8,128)}, f32[256,256]{1,0:T(8,128)}), (f32[1024,256]{1,0:T(8,128)}, f32[256,256]{0,1:T(8,128)}, f32[256,256]{1,0:T(8,128)})) %all-reduce.3.cloned.1.call-update) | async-done | bytes 1572880 | tf_op jit(solution)/shard_map/psum | solution.py:50
  655.6 0.8 constant_dynamic-slice_fusion
  656.4 6.8 %scatter_custom_fusion.1 = f32[2048,256]{1,0:T(8,128)S(1)} fusion(f32[2048,256]{1,0:T(8,128)S(1)} %convolution_add_fusion, s32[544]{0:T(1024)S(1)} %add_reduce_fusion, f32[512,256]{1,0:T(8,128)S(1)} %bitcast_convert_fusion, f32[]{:T(128)} %constant.6, f32[32,256]{1,0:T(8,128)S(1)} %constant_dynamic-slice_fusion), kind=kCustom, calls=%fused_computation.27 | custom fusion | flops 278528 | bytes 2654212 | tf_op jit(solution)/shard_map/add | solution.py:59
  663.2 0.0 copy-start.6
  663.2 0.0 copy-start.5
  663.2 1.1 convert_element_type.36
  664.3 0.0 copy-done.6
  664.3 0.8 copy.15
  665.1 0.0 copy-done.5
  665.1 0.7 copy.20
  (6 shorter events, 0.1 us)
Async XLA Ops:
  7.2 494.1 %copy-start = (bf16[256,256]{1,0:T(8,128)(2,1)S(1)}, bf16[256,256]{1,0:T(8,128)(2,1)}, u32[]{:S(2)}) copy-start(bf16[256,256]{1,0:T(8,128)(2,1)} %param.10) | copy-start | bytes 393220
  7.2 11.7 %copy-start.3 = (s32[65536]{0:T(1024)S(1)}, s32[65536]{0:T(1024)}, u32[]{:S(2)}) copy-start(s32[65536]{0:T(1024)} %param.14) | copy-start | bytes 786436
  7.2 11.7 %copy-start.4 = (s32[65536]{0:T(1024)S(1)}, s32[65536]{0:T(1024)}, u32[]{:S(2)}) copy-start(s32[65536]{0:T(1024)} %param.15) | copy-start | bytes 786436
  11.5 476.3 %all-to-all-start = ((bf16[32,16,256]{2,1,0:T(8,128)(2,1)}), bf16[32,16,256]{2,1,0:T(8,128)(2,1)S(1)}, u32[]{:S(2)}, u32[]{:S(2)}) async-start(bf16[32,16,256]{2,1,0:T(8,128)(2,1)} %bitcast), calls=%async_computation | async-start | bytes 524288 | tf_op jit(solution)/shard_map/all_to_all | solution.py:16
  18.8 636.8 %all-reduce.3.cloned.1.call-start = ((), (), s32[]{:S(2)}) async-start(), calls=%async_computation.2 | async-start | bytes 3145728 | tf_op jit(solution)/shard_map/psum | solution.py:50
  402.3 11.1 %copy-start.8 = (s32[32]{0:T(128)S(1)}, s32[32]{0:T(128)}, u32[]{:S(2)}) copy-start(s32[32]{0:T(128)} %param.12) | copy-start | bytes 388
  402.3 11.2 %copy-start.1 = (bf16[2048,256]{1,0:T(8,128)(2,1)S(1)}, bf16[2048,256]{1,0:T(8,128)(2,1)}, u32[]{:S(2)}) copy-start(bf16[2048,256]{1,0:T(8,128)(2,1)} %param.8) | copy-start | bytes 3145732
  402.3 83.7 %copy-start.2 = (bf16[256,256]{1,0:T(8,128)(2,1)S(1)}, bf16[256,256]{1,0:T(8,128)(2,1)}, u32[]{:S(2)}) copy-start(bf16[256,256]{1,0:T(8,128)(2,1)} %param.9) | copy-start | bytes 393220
  521.7 6.7 copy-start.7
  525.8 15.5 %all-to-all-start.1 = ((bf16[32,16,256]{2,1,0:T(8,128)(2,1)}), bf16[32,16,256]{2,1,0:T(8,128)(2,1)S(1)}, u32[]{:S(2)}, u32[]{:S(2)}) async-start(bf16[32,16,256]{2,1,0:T(8,128)(2,1)} %bitcast.4), calls=%async_computation.1 | async-start | bytes 524288 | tf_op jit(solution)/shard_map/all_to_all | solution.py:54
  663.2 1.1 copy-start.6
  663.2 1.9 copy-start.5
Sparse Core Ops, SparseCore 0:
  524.1 131.4 all-reduce.2
where the time goes:
time: 674 us; the launch traced here: 673 us
  other arithmetic  373 us (55%)
  waiting for transfers between devices  125 us (19%)
  blocking collectives  71.9 us (11%)
  local copies, waits for them, and re-layouts  41 us (6%)
  matrix products  37.8 us (6%)
  between operations  14.2 us (2%)
  starting transfers between devices  9.92 us (1%)
    scatter-add x1, other arithmetic, body(): counts = jnp.zeros((vcount * slot_count,), jnp.float32).at[flat_index].ad...  353 us
    psum x1, waiting for transfers between devices, body(): hub_whole = lax.psum(hub_part, ('dom', 'sub'))  114 us
    all_gather x1, blocking collectives, body(): hubs = lax.all_gather(feats[hub_rows], ('dom', 'sub'), axis=0, tiled=True)  71.9 us
    reshape x1, local copies, waits for them, and re-layouts, body(): counts = jnp.zeros((vcount * slot_count,), jnp.float32).at[flat_index].ad...  30.4 us
    dot_general x1, matrix products, body(): lax.dot_general(adjacency, dmsg, (((0,), (0,)), ((), ())), preferred_elem...  14.1 us
  transfers between devices with their start and end apart: 3, of which 2 were waited for; matrix products, arithmetic and copies ran while one was open for 60% of the time, Pallas kernels for 0%

commit v1 on v0

v1 whole, which is shorter than its diff:
```python
import functools
import math

import jax
import jax.numpy as jnp
from jax import lax
from jax.experimental import pallas as pl
from jax.experimental.pallas import tpu as pltpu
from jax.sharding import PartitionSpec as P

AXES = ("dom", "sub")
T = 256
LANES = 128


def one_hot_rows(index_row, base, rows):
    lane_index = lax.broadcasted_iota(jnp.int32, (rows, index_row.shape[1]), 0)
    return (lane_index == (index_row - base)).astype(jnp.float32).astype(jnp.bfloat16)


def outer_nt(a, b):
    return lax.dot_general(a, b, (((1,), (1,)), ((), ())), preferred_element_type=jnp.float32)


def outer_tn(a, b):
    return lax.dot_general(a, b, (((0,), (0,)), ((), ())), preferred_element_type=jnp.float32)


def mm(a, b):
    return jnp.dot(a, b, preferred_element_type=jnp.float32)


def layer_kernel(
    first_ref, last_ref, flag_ref,
    keys_ref, feats_ref, remote_ref, ws_ref, wn_ref, cot_ref,
    out_ref, base_ref, back_ref, gs_ref, gn_ref,
    adj_ref, slot_ref, deg_ref, tile_ref,
    *, own_tiles, all_tiles, window, unroll,
):
    block = pl.program_id(0)
    steps = pl.num_programs(0)
    key_rows = keys_ref.shape[0]

    def tile_part(tile, row, count):
        left = []
        right = []
        for q in range(count):
            keys = keys_ref[pl.ds(row + q, 1), :]
            left.append(one_hot_rows(keys >> 8, tile * T, T))
            right.append(one_hot_rows(keys & 255, 0, T))
        return outer_nt(jnp.concatenate(left, axis=1), jnp.concatenate(right, axis=1))

    deg_ref[...] = jnp.zeros_like(deg_ref)

    def build(j, carry):
        tile = block * all_tiles + j
        start = jnp.minimum(first_ref[tile], key_rows - window)
        counts = tile_part(tile, start, window)
        deg_ref[...] += counts[:, :LANES] + counts[:, LANES:]
        adj_ref[:, pl.ds(pl.multiple_of(j * T, T), T)] = counts.astype(jnp.bfloat16)
        return carry

    lax.fori_loop(0, all_tiles, build, 0, unroll=unroll)

    @pl.when(flag_ref[block] > 0)
    def _():
        def rest(j, carry):
            tile = block * all_tiles + j
            start = jnp.minimum(first_ref[tile], key_rows - window)
            stop = last_ref[tile]

            @pl.when(stop > start + window)
            def _():
                tile_ref[...] = tile_part(tile, start, window)

                def more(row, inner):
                    counts = tile_part(tile, row, 1)
                    deg_ref[...] += counts[:, :LANES] + counts[:, LANES:]
                    tile_ref[...] += counts
                    return inner

                lax.fori_loop(start + window, stop, more, 0)
                adj_ref[:, pl.ds(pl.multiple_of(j * T, T), T)] = tile_ref[...].astype(jnp.bfloat16)

            return carry

        lax.fori_loop(0, all_tiles, rest, 0)

    own = own_tiles * T
    total = mm(adj_ref[:, :own], feats_ref[...]) + mm(adj_ref[:, own:], remote_ref[...])
    degree = jnp.sum(deg_ref[...], axis=1, keepdims=True)
    inverse = 1.0 / jnp.maximum(degree, 1.0)
    mean = (total * inverse).astype(jnp.bfloat16)
    mine = feats_ref[pl.ds(pl.multiple_of(block * T, T), T), :]
    pre = mm(mine, ws_ref[...]) + mm(mean, wn_ref[...])
    sig = jax.nn.sigmoid(pre)
    out_ref[...] = (pre * sig).astype(jnp.bfloat16)
    slope = sig * (1.0 + pre * (1.0 - sig))
    grad_pre = (cot_ref[...].astype(jnp.float32) * slope).astype(jnp.bfloat16)

    part_self = outer_tn(mine, grad_pre)
    part_neigh = outer_tn(mean, grad_pre)

    @pl.when(block == 0)
    def _():
        gs_ref[...] = part_self
        gn_ref[...] = part_neigh
        slot_ref[...] = jnp.zeros_like(slot_ref)

    @pl.when(block > 0)
    def _():
        gs_ref[...] += part_self
        gn_ref[...] += part_neigh

    base_ref[pl.ds(pl.multiple_of(block * T, T), T), :] = outer_nt(grad_pre, ws_ref[...])
    dmsg = outer_nt(grad_pre, wn_ref[...]) * inverse
    dmsg_t = dmsg.T.astype(jnp.bfloat16)

    def spread(j, carry):
        cols = pl.ds(pl.multiple_of(j * T, T), T)
        slot_ref[:, cols] += mm(dmsg_t, adj_ref[:, cols])
        return carry

    lax.fori_loop(0, all_tiles, spread, 0, unroll=2)

    @pl.when(block == steps - 1)
    def _():
        def own_rows(j, carry):
            at = pl.ds(pl.multiple_of(j * T, T), T)
            base_ref[at, :] += slot_ref[:, at].T
            return carry

        lax.fori_loop(0, own_tiles, own_rows, 0)

        def far_rows(j, carry):
            at = pl.ds(pl.multiple_of(j * T, T), T)
            cols = pl.ds(pl.multiple_of(own + j * T, T), T)
            back_ref[at, :] = slot_ref[:, cols].T.astype(jnp.bfloat16)
            return carry

        lax.fori_loop(0, all_tiles - own_tiles, far_rows, 0)


def finish_kernel(index_ref, base_ref, back_ref, out_ref):
    block = pl.program_id(0)
    pick = one_hot_rows(index_ref[...], block * T, T)
    out_ref[...] = (base_ref[...] + mm(pick, back_ref[...])).astype(jnp.bfloat16)


def body(feats, w_self, w_neigh, cotangent, hub_rows, send_rows, edge_src, edge_dst):
    devices = lax.axis_size("dom") * lax.axis_size("sub")
    vcount, width = feats.shape
    edges = edge_src.shape[0]
    hub_dev = hub_rows.shape[0]
    cap = send_rows.shape[0] // devices
    pack = hub_dev + cap
    far = devices * pack
    slots = vcount + far
    own_tiles = vcount // T
    all_tiles = slots // T
    tiles = own_tiles * all_tiles
    key_rows = edges // LANES

    send_table = send_rows.reshape(devices, cap)
    hub_out = jnp.broadcast_to(feats[hub_rows][None], (devices, hub_dev, width))
    halo_out = feats[send_rows].reshape(devices, cap, width)
    outgoing = jnp.concatenate([hub_out, halo_out], axis=1)
    remote = lax.all_to_all(outgoing, AXES, split_axis=0, concat_axis=0, tiled=True)
    remote = remote.reshape(far, width)

    hub_at = edge_src - vcount
    halo_at = hub_at - devices * hub_dev
    hub_slot = vcount + (hub_at // hub_dev) * pack + hub_at % hub_dev
    halo_slot = vcount + (halo_at // cap) * pack + hub_dev + halo_at % cap
    slot = jnp.where(hub_at < 0, edge_src, jnp.where(halo_at < 0, hub_slot, halo_slot))
    tile_id = (edge_dst // T) * all_tiles + slot // T
    key = (tile_id * T + edge_dst % T) * T + slot % T
    keys = lax.sort(key, is_stable=False).reshape(key_rows, LANES)
    heads = keys[:, 0]
    limits = jnp.arange(tiles + 1, dtype=jnp.int32) * (T * T)
    below = jnp.sum((heads[None, :] < limits[:, None]).astype(jnp.int32), axis=1)
    first = jnp.maximum(below[:-1] - 1, 0)
    last = below[1:]
    average = edges / tiles
    window = min(key_rows, math.ceil((average + LANES + 2.0 * math.sqrt(average)) / LANES))
    over = (last > jnp.minimum(first, key_rows - window) + window).astype(jnp.int32)
    flags = jnp.max(over.reshape(own_tiles, all_tiles), axis=1)

    whole = lambda b, *_: (0, 0)
    by_block = lambda b, *_: (b, 0)
    f32 = jnp.float32
    bf16 = jnp.bfloat16
    layer_out, base, back, part_self, part_neigh = pl.pallas_call(
        functools.partial(
            layer_kernel, own_tiles=own_tiles, all_tiles=all_tiles, window=window, unroll=2
        ),
        name="layer",
        out_shape=(
            jax.ShapeDtypeStruct((vcount, width), bf16),
            jax.ShapeDtypeStruct((vcount, width), f32),
            jax.ShapeDtypeStruct((far, width), bf16),
            jax.ShapeDtypeStruct((width, width), f32),
            jax.ShapeDtypeStruct((width, width), f32),
        ),
        grid_spec=pltpu.PrefetchScalarGridSpec(
            num_scalar_prefetch=3,
            grid=(own_tiles,),
            in_specs=[
                pl.BlockSpec((key_rows, LANES), whole),
                pl.BlockSpec((vcount, width), whole),
                pl.BlockSpec((far, width), whole),
                pl.BlockSpec((width, width), whole),
                pl.BlockSpec((width, width), whole),
                pl.BlockSpec((T, width), by_block),
            ],
            out_specs=[
                pl.BlockSpec((T, width), by_block),
                pl.BlockSpec((vcount, width), whole),
                pl.BlockSpec((far, width), whole),
                pl.BlockSpec((width, width), whole),
                pl.BlockSpec((width, width), whole),
            ],
            scratch_shapes=[
                pltpu.VMEM((T, slots), bf16),
                pltpu.VMEM((width, slots), f32),
                pltpu.VMEM((T, LANES), f32),
                pltpu.VMEM((T, T), f32),
            ],
        ),
        compiler_params=pltpu.CompilerParams(
            dimension_semantics=("arbitrary",), vmem_limit_bytes=48 << 20
        ),
    )(first, last, flags, keys, feats, remote, w_self, w_neigh, cotangent)

    parts = jnp.concatenate([part_self, part_neigh], axis=0)
    share = parts.shape[0] // devices
    parts = parts.reshape(devices, share, width)
    parts = lax.all_to_all(parts, AXES, split_axis=0, concat_axis=0, tiled=True)
    mine = jnp.sum(parts, axis=0)
    grads = jnp.broadcast_to(mine[None], (devices, share, width))
    grads = lax.all_to_all(grads, AXES, split_axis=0, concat_axis=0, tiled=True)
    grads = grads.reshape(2 * width, width)

    returned = lax.all_to_all(
        back.reshape(devices, pack, width), AXES, split_axis=0, concat_axis=0, tiled=True
    ).reshape(far, width)
    index = jnp.concatenate(
        [jnp.broadcast_to(hub_rows[None], (devices, hub_dev)), send_table], axis=1
    ).reshape(1, far)
    grad_feats = pl.pallas_call(
        finish_kernel,
        name="finish",
        out_shape=jax.ShapeDtypeStruct((vcount, width), bf16),
        grid=(own_tiles,),
        in_specs=[
            pl.BlockSpec((1, far), lambda b: (0, 0)),
            pl.BlockSpec((T, width), lambda b: (b, 0)),
            pl.BlockSpec((far, width), lambda b: (0, 0)),
        ],
        out_specs=pl.BlockSpec((T, width), lambda b: (b, 0)),
        compiler_params=pltpu.CompilerParams(
            dimension_semantics=("arbitrary",), vmem_limit_bytes=32 << 20
        ),
    )(index, base, returned)
    return (layer_out, grad_feats, grads[:width], grads[width:])


def solution(mesh):
    return jax.shard_map(
        body,
        mesh=mesh,
        in_specs=(
            P(AXES, None),
            P(),
            P(),
            P(AXES, None),
            P(AXES),
            P(AXES),
            P(AXES),
            P(AXES),
        ),
        out_specs=(P(AXES, None), P(AXES, None), P(), P()),
        check_vma=False,
    )
```

time: 674 us -> 159 us (0.24)
  other arithmetic: 373 us -> 15.4 us
  waiting for transfers between devices: 125 us -> 42.3 us
  Pallas kernels: 0 us -> 61.5 us
  blocking collectives: 71.9 us -> 18.4 us
  matrix products: 37.8 us -> 0 us
  local copies, waits for them, and re-layouts: 41 us -> 7.04 us
  between operations: 14.2 us -> 0.78 us
    scatter-add x1 -> x0, other arithmetic: 353 us -> none  [body(): counts = jnp.zeros((vcount * slot_count,), jnp.float32).at[flat_index].ad...]
    psum x1 -> x0, waiting for transfers between devices: 114 us -> none  [body(): hub_whole = lax.psum(hub_part, ('dom', 'sub'))]
    all_gather x1 -> x0, blocking collectives: 71.9 us -> none  [body(): hubs = lax.all_gather(feats[hub_rows], ('dom', 'sub'), axis=0, tiled=True)]
    pallas_call x0 -> x2, Pallas kernels: none -> 61.5 us  [the longest x1 57 us: body(): pl.pallas_call(functools.partial(layer_kernel, own_tiles=own_tiles, all_t...]
    dot_general x7 -> x0, matrix products: 37.8 us -> none  [the longest x1 14.1 us: body(): lax.dot_general(adjacency, dmsg, (((0,), (0,)), ((), ())), preferred_elem...]
    all_to_all x2 -> x3, waiting for transfers between devices: 10.6 us -> 42.3 us  [the longest x1 21.9 us: body(): lax.all_to_all(back.reshape(devices, pack, width), AXES, split_axis=0, co...]
    reshape x1 -> x2, local copies, waits for them, and re-layouts: 30.4 us -> 0.16 us  [the longest x1 0.08 us: body(): index = jnp.concatenate([jnp.broadcast_to(hub_rows[None], (devices, hub_d...]
    all_to_all x0 -> x1, blocking collectives: none -> 18.4 us  [body(): parts = lax.all_to_all(parts, AXES, split_axis=0, concat_axis=0, tiled=True)]
  transfers between devices with their start and end apart: 3 -> 3, of which waited for: 2 -> 3; matrix products, arithmetic and copies ran while one was open for 60% -> 8% of each run, Pallas kernels for 0% -> 3%
where the time goes in v1:
time: 159 us; the launch traced here: 158 us
  Pallas kernels  61.5 us (39%)
  waiting for transfers between devices  42.3 us (27%)
  blocking collectives  18.4 us (12%)
  other arithmetic  15.4 us (10%)
  starting transfers between devices  12.7 us (8%)
  local copies, waits for them, and re-layouts  7.04 us (4%)
    pallas_call x1, Pallas kernels, body(): pl.pallas_call(functools.partial(layer_kernel, own_tiles=own_tiles, all_t...  57 us
    all_to_all x1, waiting for transfers between devices, body(): lax.all_to_all(back.reshape(devices, pack, width), AXES, split_axis=0, co...  21.9 us
    all_to_all x1, blocking collectives, body(): parts = lax.all_to_all(parts, AXES, split_axis=0, concat_axis=0, tiled=True)  18.4 us
    all_to_all x1, waiting for transfers between devices, body(): grads = lax.all_to_all(grads, AXES, split_axis=0, concat_axis=0, tiled=True)  11.6 us
    sort x1, other arithmetic, body(): keys = lax.sort(key, is_stable=False).reshape(key_rows, LANES)  9.79 us
    all_to_all x1, waiting for transfers between devices, body(): lax.all_to_all(outgoing, AXES, split_axis=0, concat_axis=0, tiled=True)  8.79 us
    all_to_all x1, starting transfers between devices, body(): lax.all_to_all(outgoing, AXES, split_axis=0, concat_axis=0, tiled=True)  7.3 us
    pallas_call x1, Pallas kernels, body(): pl.pallas_call(finish_kernel, name='finish', out_shape=jax.ShapeDtypeStru...  4.52 us
  transfers between devices with their start and end apart: 3, of which 3 were waited for; matrix products, arithmetic and copies ran while one was open for 8% of the time, Pallas kernels for 3%

profile of v1, /device:TPU:0, one launch (start us, length us, event | category | flops | bytes accessed | tf_op | source)
XLA Modules:
  0.0 158.1 jit_solution(5350395623996227385)
XLA Ops:
  0.6 0.7 compare_select_fusion.1
  1.3 0.7 compare_select_fusion
  2.0 2.0 %gather_fusion = bf16[32,256]{1,0:T(8,128)(2,1)S(1)} fusion(bf16[2048,256]{1,0:T(8,128)(2,1)} %feats_ref.1, s32[1024]{0:T(1024)S(1)} %pad_clamp_fusion.1), kind=kCustom, calls=%fused_computation | custom fusion | bytes 32896 | tf_op jit(solution)/shard_map/gather | solution.py:165
  4.0 2.9 %gather_fusion.1 = bf16[512,256]{1,0:T(8,128)(2,1)S(1)} fusion(bf16[2048,256]{1,0:T(8,128)(2,1)} %feats_ref.1, s32[1024]{0:T(1024)S(1)} %pad_clamp_fusion), kind=kCustom, calls=%fused_computation.1 | custom fusion | bytes 526336 | tf_op jit(solution)/shard_map/gather | solution.py:166
  6.9 0.1 broadcast_in_dim.11
  6.9 0.0 copy-start.6
  7.0 0.9 pad_maximum_fusion
  7.9 0.0 copy-start
  7.9 0.0 copy-start.2
  7.9 0.0 copy-start.4
  7.9 0.0 copy-start.5
  7.9 7.3 %all-to-all-start = ((bf16[32,48,256]{2,1,0:T(8,128)(2,1)}), bf16[32,48,256]{2,1,0:T(8,128)(2,1)S(1)}, u32[]{:S(2)}, u32[]{:S(2)}) async-start(bf16[32,48,256]{2,1,0:T(8,128)(2,1)} %pad_maximum_fusion), calls=%async_computation | async-start | bytes 1572864 | tf_op jit(solution)/shard_map/all_to_all | solution.py:168
  15.2 0.0 copy-done.6
  15.2 2.7 %fusion.5 = s32[65536]{0:T(1024)} fusion(s32[65536]{0:T(1024)S(1)} %copy-done.6, s32[65536]{0:T(1024)} %param.14), kind=kLoop, calls=%fused_computation.29 | loop fusion | flops 6029312 | bytes 786432 | tf_op jit(solution)/shard_map/add | solution.py:177
  17.9 9.8 %sort.7 = s32[65536]{0:T(1024)S(1)} sort(s32[65536]{0:T(1024)} %fusion.5), dimensions={0}, to_apply=%region_0.1 | sort | flops 1048576 | bytes 524288 | tf_op jit(solution)/shard_map/sort | solution.py:178
  27.7 0.1 slice_reduce_fusion
  27.8 0.2 convert_reduce_fusion
  28.0 0.1 compare_convert_fusion
  28.1 0.1 reshape.62
  28.2 0.1 reduce_max.9.flag_ref
  28.3 0.1 fusion.31
  28.4 8.8 %all-to-all-done = bf16[32,48,256]{2,1,0:T(8,128)(2,1)S(1)} async-done(((bf16[32,48,256]{2,1,0:T(8,128)(2,1)}), bf16[32,48,256]{2,1,0:T(8,128)(2,1)S(1)}, u32[]{:S(2)}, u32[]{:S(2)}) %all-to-all-start) | async-done | bytes 786464 | tf_op jit(solution)/shard_map/all_to_all | solution.py:168
  37.2 0.0 copy-done
  37.2 0.0 copy-done.2
  37.2 0.0 copy-done.4
  37.2 0.0 copy-done.5
  37.2 57.0 %layer.1 = (bf16[2048,256]{1,0:T(8,128)(2,1)}, f32[2048,256]{1,0:T(8,128)}, bf16[1536,256]{1,0:T(8,128)(2,1)S(1)}, f32[256,256]{1,0:T(8,128)S(1)}, f32[256,256]{1,0:T(8,128)S(1)}) custom-call(s32[112]{0:T(128)S(1)} %get-tuple-element.17.first_ref, s32[112]{0:T(128)S(1)} %get-tuple-element.16.last_ref, s32[8]{0:T(128)S(1)} %reduce_max.9.flag_ref, ...), custom_call_target="tpu_custom_call" | custom-call | tf_op jit(solution)/shard_map/layer/pallas_call | solution.py:193
  94.2 0.0 copy-start.3
  94.2 18.4 %all_to_all.20 = f32[32,16,256]{2,1,0:T(8,128)S(1)} all-to-all(f32[32,16,256]{2,1,0:T(8,128)S(1)} %bitcast.13), channel_id=1, replica_groups=mesh['dom'=4,'sub'=8] {'dom','sub'}, dimensions={0} | all-to-all | bytes 1048576 | tf_op jit(solution)/shard_map/all_to_all | solution.py:238
  112.7 0.0 copy-done.3
  112.7 0.0 copy-start.7
  112.7 0.0 copy-start.8
  112.7 0.0 copy-start.1
  112.7 2.8 %all-to-all-start.1 = ((bf16[32,48,256]{2,1,0:T(8,128)(2,1)}), bf16[32,48,256]{2,1,0:T(8,128)(2,1)S(1)}, u32[]{:S(2)}, u32[]{:S(2)}) async-start(bf16[32,48,256]{2,1,0:T(8,128)(2,1)} %bitcast.12), calls=%async_computation.1 | async-start | bytes 1572864 | tf_op jit(solution)/shard_map/all_to_all | solution.py:244
  115.5 21.9 %all-to-all-done.1 = bf16[32,48,256]{2,1,0:T(8,128)(2,1)S(1)} async-done(((bf16[32,48,256]{2,1,0:T(8,128)(2,1)}), bf16[32,48,256]{2,1,0:T(8,128)(2,1)S(1)}, u32[]{:S(2)}, u32[]{:S(2)}) %all-to-all-start.1) | async-done | bytes 786464 | tf_op jit(solution)/shard_map/all_to_all | solution.py:244
  137.4 0.9 broadcast_in_dim.14
  138.3 2.6 %all-to-all-start.3 = ((f32[32,16,256]{2,1,0:T(8,128)}), f32[32,16,256]{2,1,0:T(8,128)S(1)}, u32[]{:S(2)}, u32[]{:S(2)}) async-start(f32[32,16,256]{2,1,0:T(8,128)} %broadcast_in_dim.14), calls=%async_computation.3 | async-start | bytes 1048576 | tf_op jit(solution)/shard_map/all_to_all | solution.py:241
  140.9 0.0 copy-done.7
  140.9 0.1 reshape.57
  141.0 0.0 copy-done.8
  141.0 0.1 pad_add_fusion
  141.1 0.1 reshape.58.index_ref
  141.2 0.0 copy-done.1
  141.2 4.5 %finish.1 = bf16[2048,256]{1,0:T(8,128)(2,1)} custom-call(s32[1,1536]{1,0:T(1,128)S(1)} %reshape.58.index_ref, f32[2048,256]{1,0:T(8,128)S(1)} %copy-done.1, bf16[1536,256]{1,0:T(8,128)(2,1)S(1)} %bitcast.9), custom_call_target="tpu_custom_call" | custom-call | tf_op jit(solution)/shard_map/finish/pallas_call | solution.py:250
  145.7 11.6 %all-to-all-done.3 = f32[32,16,256]{2,1,0:T(8,128)S(1)} async-done(((f32[32,16,256]{2,1,0:T(8,128)}), f32[32,16,256]{2,1,0:T(8,128)S(1)}, u32[]{:S(2)}, u32[]{:S(2)}) %all-to-all-start.3) | async-done | bytes 524320 | tf_op jit(solution)/shard_map/all_to_all | solution.py:241
  157.3 0.8 fusion.30
  (6 shorter events, 0.1 us)
Async XLA Ops:
  6.9 8.3 %copy-start.6 = (s32[65536]{0:T(1024)S(1)}, s32[65536]{0:T(1024)}, u32[]{:S(2)}) copy-start(s32[65536]{0:T(1024)} %param.15) | copy-start | bytes 786436
  7.9 29.3 %copy-start = (bf16[2048,256]{1,0:T(8,128)(2,1)S(1)}, bf16[2048,256]{1,0:T(8,128)(2,1)}, u32[]{:S(2)}) copy-start(bf16[2048,256]{1,0:T(8,128)(2,1)} %feats_ref.1) | copy-start | bytes 3145732
  7.9 29.3 %copy-start.2 = (bf16[2048,256]{1,0:T(8,128)(2,1)S(1)}, bf16[2048,256]{1,0:T(8,128)(2,1)}, u32[]{:S(2)}) copy-start(bf16[2048,256]{1,0:T(8,128)(2,1)} %cot_ref.1) | copy-start | bytes 3145732
  7.9 29.3 %copy-start.4 = (bf16[256,256]{1,0:T(8,128)(2,1)S(1)}, bf16[256,256]{1,0:T(8,128)(2,1)}, u32[]{:S(2)}) copy-start(bf16[256,256]{1,0:T(8,128)(2,1)} %ws_ref.1) | copy-start | bytes 393220
  7.9 29.3 %copy-start.5 = (bf16[256,256]{1,0:T(8,128)(2,1)S(1)}, bf16[256,256]{1,0:T(8,128)(2,1)}, u32[]{:S(2)}) copy-start(bf16[256,256]{1,0:T(8,128)(2,1)} %wn_ref.1) | copy-start | bytes 393220
  7.9 29.3 %all-to-all-start = ((bf16[32,48,256]{2,1,0:T(8,128)(2,1)}), bf16[32,48,256]{2,1,0:T(8,128)(2,1)S(1)}, u32[]{:S(2)}, u32[]{:S(2)}) async-start(bf16[32,48,256]{2,1,0:T(8,128)(2,1)} %pad_maximum_fusion), calls=%async_computation | async-start | bytes 1572864 | tf_op jit(solution)/shard_map/all_to_all | solution.py:168
  94.2 18.5 %copy-start.3 = (bf16[1536,256]{1,0:T(8,128)(2,1)}, bf16[1536,256]{1,0:T(8,128)(2,1)S(1)}, u32[]{:S(2)}) copy-start(bf16[1536,256]{1,0:T(8,128)(2,1)S(1)} %get-tuple-element.11) | copy-start | bytes 2359300
  112.7 28.2 %copy-start.7 = (s32[512]{0:T(512)S(1)}, s32[512]{0:T(512)}, u32[]{:S(2)}) copy-start(s32[512]{0:T(512)} %param.13) | copy-start | bytes 6148
  112.7 28.3 %copy-start.8 = (s32[32]{0:T(128)S(1)}, s32[32]{0:T(128)}, u32[]{:S(2)}) copy-start(s32[32]{0:T(128)} %param.12) | copy-start | bytes 388
  112.7 28.5 %copy-start.1 = (f32[2048,256]{1,0:T(8,128)S(1)}, f32[2048,256]{1,0:T(8,128)}, u32[]{:S(2)}) copy-start(f32[2048,256]{1,0:T(8,128)} %get-tuple-element.10.base_ref) | copy-start | bytes 6291460
  112.7 24.8 %all-to-all-start.1 = ((bf16[32,48,256]{2,1,0:T(8,128)(2,1)}), bf16[32,48,256]{2,1,0:T(8,128)(2,1)S(1)}, u32[]{:S(2)}, u32[]{:S(2)}) async-start(bf16[32,48,256]{2,1,0:T(8,128)(2,1)} %bitcast.12), calls=%async_computation.1 | async-start | bytes 1572864 | tf_op jit(solution)/shard_map/all_to_all | solution.py:244
  138.3 19.0 %all-to-all-start.3 = ((f32[32,16,256]{2,1,0:T(8,128)}), f32[32,16,256]{2,1,0:T(8,128)S(1)}, u32[]{:S(2)}, u32[]{:S(2)}) async-start(f32[32,16,256]{2,1,0:T(8,128)} %broadcast_in_dim.14), calls=%async_computation.3 | async-start | bytes 1048576 | tf_op jit(solution)/shard_map/all_to_all | solution.py:241

commit v2 on v1

v2 whole, which is shorter than its diff:
```python
import functools
import math

import jax
import jax.numpy as jnp
from jax import lax
from jax.experimental import pallas as pl
from jax.experimental.pallas import tpu as pltpu
from jax.sharding import PartitionSpec as P

AXES = ("dom", "sub")
T = 256
LANES = 128
F8 = jnp.float8_e4m3fn


def outer_nt(a, b):
    return lax.dot_general(a, b, (((1,), (1,)), ((), ())), preferred_element_type=jnp.float32)


def outer_tn(a, b):
    return lax.dot_general(a, b, (((0,), (0,)), ((), ())), preferred_element_type=jnp.float32)


def mm(a, b):
    return jnp.dot(a, b, preferred_element_type=jnp.float32)


def counts_kernel(first_ref, last_ref, flag_ref, keys_ref, adj_ref, deg_ref, tile_ref,
                  *, all_tiles, window, unroll):
    block = pl.program_id(0)
    key_rows = keys_ref.shape[0]
    ids = (lax.broadcasted_iota(jnp.int32, (T, LANES), 0) - 128).astype(jnp.int8)
    none = jnp.zeros((T, LANES), F8)
    ones = jnp.ones((T, LANES), F8)

    def match(low):
        return ids == jnp.broadcast_to((low - 128).astype(jnp.int8), (T, LANES))

    def tile_part(tile, row, count):
        left = []
        right = []
        for q in range(count):
            keys = keys_ref[pl.ds(row + q, 1), :]
            inside = jnp.where((keys >> 16) == tile, 1.0, 0.0).astype(F8)
            left.append(
                jnp.where(match((keys >> 8) & 255), jnp.broadcast_to(inside, (T, LANES)), none)
            )
            right.append(jnp.where(match(keys & 255), ones, none))
        return outer_nt(jnp.concatenate(left, axis=1), jnp.concatenate(right, axis=1))

    deg_ref[...] = jnp.zeros_like(deg_ref)

    def build(j, carry):
        tile = block * all_tiles + j
        start = jnp.minimum(first_ref[tile], key_rows - window)
        counts = tile_part(tile, start, window)
        deg_ref[...] += counts[:, :LANES] + counts[:, LANES:]
        adj_ref[:, pl.ds(pl.multiple_of(j * T, T), T)] = counts.astype(jnp.bfloat16)
        return carry

    lax.fori_loop(0, all_tiles, build, 0, unroll=unroll)

    @pl.when(flag_ref[block] > 0)
    def _():
        def rest(j, carry):
            tile = block * all_tiles + j
            start = jnp.minimum(first_ref[tile], key_rows - window)
            stop = last_ref[tile]

            @pl.when(stop > start + window)
            def _():
                tile_ref[...] = tile_part(tile, start, window)

                def more(row, inner):
                    counts = tile_part(tile, row, 1)
                    deg_ref[...] += counts[:, :LANES] + counts[:, LANES:]
                    tile_ref[...] += counts
                    return inner

                lax.fori_loop(start + window, stop, more, 0)
                adj_ref[:, pl.ds(pl.multiple_of(j * T, T), T)] = tile_ref[...].astype(jnp.bfloat16)

            return carry

        lax.fori_loop(0, all_tiles, rest, 0)


def forward_kernel(adj_ref, deg_ref, feats_ref, remote_ref, ws_ref, wn_ref, cot_ref,
                   out_ref, g_ref, dmsg_ref, grads_ref):
    block = pl.program_id(0)
    rows, width = out_ref.shape
    own = feats_ref.shape[0]
    total = mm(adj_ref[:, :own], feats_ref[...]) + mm(adj_ref[:, own:], remote_ref[...])
    degree = jnp.sum(deg_ref[...], axis=1, keepdims=True)
    inverse = 1.0 / jnp.maximum(degree, 1.0)
    mean = (total * inverse).astype(jnp.bfloat16)
    mine = feats_ref[pl.ds(pl.multiple_of(block * rows, rows), rows), :]
    pre = mm(mine, ws_ref[...]) + mm(mean, wn_ref[...])
    sig = jax.nn.sigmoid(pre)
    out_ref[...] = (pre * sig).astype(jnp.bfloat16)
    slope = sig * (1.0 + pre * (1.0 - sig))
    g = (cot_ref[...].astype(jnp.float32) * slope).astype(jnp.bfloat16)
    g_ref[...] = g
    dmsg_ref[...] = (outer_nt(g, wn_ref[...]) * inverse).astype(jnp.bfloat16)

    @pl.when(block == 0)
    def _():
        grads_ref[...] = jnp.zeros_like(grads_ref)

    grads_ref[:width, :] += outer_tn(mine, g)
    grads_ref[width:, :] += outer_tn(mean, g)


def far_kernel(adj_ref, dmsg_ref, back_ref):
    back_ref[...] = outer_tn(adj_ref[...], dmsg_ref[...]).astype(jnp.bfloat16)


def own_kernel(adj_ref, dmsg_ref, g_ref, ws_ref, base_ref):
    base_ref[...] = outer_tn(adj_ref[...], dmsg_ref[...]) + outer_nt(g_ref[...], ws_ref[...])


def finish_kernel(index_ref, base_ref, back_ref, out_ref):
    block = pl.program_id(0)
    rows = out_ref.shape[0]
    far = index_ref.shape[1]
    spot = jnp.clip(index_ref[...] - block * rows, -1, rows).astype(jnp.int16)
    ids = lax.broadcasted_iota(jnp.int16, (rows, far), 0)
    pick = jnp.where(
        ids == jnp.broadcast_to(spot, (rows, far)),
        jnp.ones((rows, far), jnp.bfloat16),
        jnp.zeros((rows, far), jnp.bfloat16),
    )
    out_ref[...] = (base_ref[...] + mm(pick, back_ref[...])).astype(jnp.bfloat16)


def all_reduce(parts, gate):
    dom = lax.axis_size("dom")
    sub = lax.axis_size("sub")
    at = lax.axis_index("dom")
    steps = []
    stride = 1
    while stride < dom:
        half = parts.shape[0] // 2
        bit = (at // stride) % 2
        pairs = [(i, i ^ stride) for i in range(dom)]
        sent = lax.dynamic_slice_in_dim(parts, (1 - bit) * half, half, 0)
        kept = lax.dynamic_slice_in_dim(parts, bit * half, half, 0)
        came = lax.ppermute(sent, "dom", pairs)
        if stride == 1:
            came, gate = lax.optimization_barrier((came, gate))
        parts = kept + came
        steps.append((bit, pairs))
        stride *= 2
    stride = 1
    while stride < sub:
        parts = parts + lax.ppermute(parts, "sub", [(i, i ^ stride) for i in range(sub)])
        stride *= 2
    parts = parts.astype(jnp.bfloat16)
    for bit, pairs in reversed(steps):
        other = lax.ppermute(parts, "dom", pairs)
        low = jnp.where(bit == 0, parts, other)
        high = jnp.where(bit == 0, other, parts)
        parts = jnp.concatenate([low, high], axis=0)
    return parts.astype(jnp.float32), gate


def call(kernel, grid, in_specs, out_specs, out_shape, name, vmem):
    return pl.pallas_call(
        kernel,
        name=name,
        grid=grid,
        in_specs=in_specs,
        out_specs=out_specs,
        out_shape=out_shape,
        compiler_params=pltpu.CompilerParams(
            dimension_semantics=("arbitrary",), vmem_limit_bytes=vmem
        ),
    )


def body(feats, w_self, w_neigh, cotangent, hub_rows, send_rows, edge_src, edge_dst):
    devices = lax.axis_size("dom") * lax.axis_size("sub")
    vcount, width = feats.shape
    edges = edge_src.shape[0]
    hub_dev = hub_rows.shape[0]
    cap = send_rows.shape[0] // devices
    pack = hub_dev + cap
    far = devices * pack
    slots = vcount + far
    own_tiles = vcount // T
    all_tiles = slots // T
    tiles = own_tiles * all_tiles
    key_rows = edges // LANES
    f32 = jnp.float32
    bf16 = jnp.bfloat16

    send_table = send_rows.reshape(devices, cap)
    hub_out = jnp.broadcast_to(feats[hub_rows][None], (devices, hub_dev, width))
    halo_out = feats[send_rows].reshape(devices, cap, width)
    outgoing = jnp.concatenate([hub_out, halo_out], axis=1)
    remote = lax.all_to_all(outgoing, AXES, split_axis=0, concat_axis=0, tiled=True)
    remote = remote.reshape(far, width)

    hub_at = edge_src - vcount
    halo_at = hub_at - devices * hub_dev
    hub_slot = vcount + (hub_at // hub_dev) * pack + hub_at % hub_dev
    halo_slot = vcount + (halo_at // cap) * pack + hub_dev + halo_at % cap
    slot = jnp.where(hub_at < 0, edge_src, jnp.where(halo_at < 0, hub_slot, halo_slot))
    tile_id = (edge_dst // T) * all_tiles + slot // T
    key = (tile_id * T + edge_dst % T) * T + slot % T
    keys = lax.sort(key, is_stable=False).reshape(key_rows, LANES)
    heads = keys[:, 0]
    limits = jnp.arange(tiles + 1, dtype=jnp.int32) * (T * T)
    below = jnp.sum((heads[None, :] < limits[:, None]).astype(jnp.int32), axis=1)
    first = jnp.maximum(below[:-1] - 1, 0)
    last = below[1:]
    average = edges / tiles
    window = min(key_rows, math.ceil((average + LANES + 2.0 * math.sqrt(average)) / LANES))
    over = (last > jnp.minimum(first, key_rows - window) + window).astype(jnp.int32)
    flags = jnp.max(over.reshape(own_tiles, all_tiles), axis=1)
    unroll = max(u for u in range(1, 17) if all_tiles % u == 0)

    adj, deg = pl.pallas_call(
        functools.partial(counts_kernel, all_tiles=all_tiles, window=window, unroll=unroll),
        name="counts",
        out_shape=(
            pltpu.HBM((vcount, slots), bf16),
            pltpu.HBM((vcount, LANES), f32),
        ),
        grid_spec=pltpu.PrefetchScalarGridSpec(
            num_scalar_prefetch=3,
            grid=(own_tiles,),
            in_specs=[pl.BlockSpec((key_rows, LANES), lambda b, *_: (0, 0))],
            out_specs=[
                pl.BlockSpec((T, slots), lambda b, *_: (b, 0)),
                pl.BlockSpec((T, LANES), lambda b, *_: (b, 0)),
            ],
            scratch_shapes=[pltpu.VMEM((T, T), f32)],
        ),
        compiler_params=pltpu.CompilerParams(
            dimension_semantics=("arbitrary",), vmem_limit_bytes=(8 << 20) + 6 * T * slots
        ),
    )(first, last, flags, keys)

    adj = pltpu.with_memory_space_constraint(adj, pltpu.HBM)
    deg = pltpu.with_memory_space_constraint(deg, pltpu.HBM)
    whole = lambda b: (0, 0)
    by_row = lambda b: (b, 0)
    rows = min(2 * T, vcount)
    layer_out, g, dmsg, parts = call(
        forward_kernel,
        (vcount // rows,),
        [
            pl.BlockSpec((rows, slots), by_row),
            pl.BlockSpec((rows, LANES), by_row),
            pl.BlockSpec((vcount, width), whole),
            pl.BlockSpec((far, width), whole),
            pl.BlockSpec((width, width), whole),
            pl.BlockSpec((width, width), whole),
            pl.BlockSpec((rows, width), by_row),
        ],
        [
            pl.BlockSpec((rows, width), by_row),
            pl.BlockSpec((rows, width), by_row),
            pl.BlockSpec((rows, width), by_row),
            pl.BlockSpec((2 * width, width), whole),
        ],
        (
            pltpu.HBM((vcount, width), bf16),
            pltpu.HBM((vcount, width), bf16),
            pltpu.HBM((vcount, width), bf16),
            jax.ShapeDtypeStruct((2 * width, width), f32),
        ),
        "forward",
        (8 << 20) + 4 * rows * slots + 4 * slots * width,
    )(adj, deg, feats, remote, w_self, w_neigh, cotangent)

    g = pltpu.with_memory_space_constraint(g, pltpu.HBM)
    dmsg = pltpu.with_memory_space_constraint(dmsg, pltpu.HBM)
    cols = 2 * T
    skip = vcount // cols
    back = call(
        far_kernel,
        (far // cols,),
        [
            pl.BlockSpec((vcount, cols), lambda j: (0, j + skip)),
            pl.BlockSpec((vcount, width), whole),
        ],
        pl.BlockSpec((cols, width), by_row),
        jax.ShapeDtypeStruct((far, width), bf16),
        "far",
        16 << 20,
    )(adj, dmsg)
    grads, back = all_reduce(parts, back)
    returned = lax.all_to_all(
        back.reshape(devices, pack, width), AXES, split_axis=0, concat_axis=0, tiled=True
    ).reshape(far, width)
    base = call(
        own_kernel,
        (vcount // cols,),
        [
            pl.BlockSpec((vcount, cols), lambda j: (0, j)),
            pl.BlockSpec((vcount, width), whole),
            pl.BlockSpec((cols, width), by_row),
            pl.BlockSpec((width, width), whole),
        ],
        pl.BlockSpec((cols, width), by_row),
        jax.ShapeDtypeStruct((vcount, width), f32),
        "own",
        16 << 20,
    )(adj, dmsg, g, w_self)

    index = jnp.concatenate(
        [jnp.broadcast_to(hub_rows[None], (devices, hub_dev)), send_table], axis=1
    ).reshape(1, far)
    grad_feats = call(
        finish_kernel,
        (own_tiles,),
        [
            pl.BlockSpec((1, far), whole),
            pl.BlockSpec((T, width), by_row),
            pl.BlockSpec((far, width), whole),
        ],
        pl.BlockSpec((T, width), by_row),
        jax.ShapeDtypeStruct((vcount, width), bf16),
        "finish",
        (8 << 20) + 8 * far * width,
    )(index, base, returned)
    return (layer_out, grad_feats, grads[:width], grads[width:])


def solution(mesh):
    return jax.shard_map(
        body,
        mesh=mesh,
        in_specs=(
            P(AXES, None),
            P(),
            P(),
            P(AXES, None),
            P(AXES),
            P(AXES),
            P(AXES),
            P(AXES),
        ),
        out_specs=(P(AXES, None), P(AXES, None), P(), P()),
        check_vma=False,
    )
```

time: 159 us -> 107 us (0.67)
  Pallas kernels: 61.5 us -> 40 us
  waiting for transfers between devices: 42.3 us -> 21.8 us
  blocking collectives: 18.4 us -> 0 us
  starting transfers between devices: 12.7 us -> 22.4 us
    pallas_call x2 -> x5, Pallas kernels: 61.5 us -> 40 us  [the longest x1 12.1 us: body(): call(forward_kernel, (vcount // rows,), [pl.BlockSpec((rows, slots), by_r...]
    all_to_all x1 -> x0, blocking collectives: 18.4 us -> none  [body(): parts = lax.all_to_all(parts, AXES, split_axis=0, concat_axis=0, tiled=True)]
    all_to_all x1, waiting for transfers between devices: 21.9 us -> 4.85 us  [body(): lax.all_to_all(back.reshape(devices, pack, width), AXES, split_axis=0, co...]
    ppermute x0 -> x7, waiting for transfers between devices: none -> 16.9 us  [the longest x2 6.75 us: all_reduce(): other = lax.ppermute(parts, 'dom', pairs)]
    all_to_all x1 -> x0, waiting for transfers between devices: 11.6 us -> none  [body(): grads = lax.all_to_all(grads, AXES, split_axis=0, concat_axis=0, tiled=True)]
    ppermute x0 -> x7, starting transfers between devices: none -> 10.9 us  [the longest x3 6.6 us: all_reduce(): lax.ppermute(parts, 'sub', [(i, i ^ stride) for i in range(sub)])]
    all_to_all x1, waiting for transfers between devices: 8.79 us -> 0.01 us  [body(): lax.all_to_all(outgoing, AXES, split_axis=0, concat_axis=0, tiled=True)]
    all_to_all x1 -> x0, starting transfers between devices: 2.6 us -> none  [body(): grads = lax.all_to_all(grads, AXES, split_axis=0, concat_axis=0, tiled=True)]
  transfers between devices with their start and end apart: 3 -> 9, of which waited for: 3 -> 5; matrix products, arithmetic and copies ran while one was open for 8% -> 13% of each run, Pallas kernels for 3% -> 22%
where the time goes in v2:
time: 107 us; the launch traced here: 106 us
  Pallas kernels  40 us (37%)
  starting transfers between devices  22.4 us (21%)
  waiting for transfers between devices  21.8 us (20%)
  other arithmetic  15.6 us (15%)
  local copies, waits for them, and re-layouts  5.68 us (5%)
    pallas_call x1, Pallas kernels, body(): call(forward_kernel, (vcount // rows,), [pl.BlockSpec((rows, slots), by_r...  12.1 us
    pallas_call x1, Pallas kernels, body(): pl.pallas_call(functools.partial(counts_kernel, all_tiles=all_tiles, wind...  10.7 us
    sort x1, other arithmetic, body(): keys = lax.sort(key, is_stable=False).reshape(key_rows, LANES)  9.79 us
    all_to_all x1, starting transfers between devices, body(): lax.all_to_all(outgoing, AXES, split_axis=0, concat_axis=0, tiled=True)  7.3 us
    pallas_call x1, Pallas kernels, body(): call(own_kernel, (vcount // cols,), [pl.BlockSpec((vcount, cols), lambda...  6.89 us
    ppermute x2, waiting for transfers between devices, all_reduce(): other = lax.ppermute(parts, 'dom', pairs)  6.75 us
    ppermute x3, starting transfers between devices, all_reduce(): lax.ppermute(parts, 'sub', [(i, i ^ stride) for i in range(sub)])  6.6 us
    ppermute x3, waiting for transfers between devices, all_reduce(): lax.ppermute(parts, 'sub', [(i, i ^ stride) for i in range(sub)])  6.18 us
  transfers between devices with their start and end apart: 9, of which 5 were waited for; matrix products, arithmetic and copies ran while one was open for 13% of the time, Pallas kernels for 22%

profile of v2, /device:TPU:0, one launch (start us, length us, event | category | flops | bytes accessed | tf_op | source)
XLA Modules:
  0.0 106.4 jit_solution(8926495958468282779)
XLA Ops:
  0.6 0.0 copy-start
  0.6 0.8 compare_select_fusion
  1.4 0.7 compare_select_fusion.1
  2.1 2.9 %gather_fusion.1 = bf16[512,256]{1,0:T(8,128)(2,1)S(1)} fusion(bf16[2048,256]{1,0:T(8,128)(2,1)} %feats_ref.1, s32[1024]{0:T(1024)S(1)} %pad_clamp_fusion), kind=kCustom, calls=%fused_computation.1 | custom fusion | bytes 526336 | tf_op jit(solution)/shard_map/gather | solution.py:200
  5.0 0.0 copy-done
  5.0 0.6 gather_fusion
  5.7 0.1 broadcast_in_dim.9
  5.7 0.0 copy-start.6
  5.7 0.9 pad_maximum_fusion
  6.7 0.0 copy-start.1
  6.7 0.0 copy-start.2
  6.7 0.0 copy-start.5
  6.7 7.3 %all-to-all-start = ((bf16[32,48,256]{2,1,0:T(8,128)(2,1)}), bf16[32,48,256]{2,1,0:T(8,128)(2,1)S(1)}, u32[]{:S(2)}, u32[]{:S(2)}) async-start(bf16[32,48,256]{2,1,0:T(8,128)(2,1)} %pad_maximum_fusion), calls=%async_computation | async-start | bytes 1572864 | tf_op jit(solution)/shard_map/all_to_all | solution.py:202
  14.0 0.0 copy-done.6
  14.0 2.7 %fusion.5 = s32[65536]{0:T(1024)} fusion(s32[65536]{0:T(1024)S(1)} %copy-done.6, s32[65536]{0:T(1024)} %param.14), kind=kLoop, calls=%fused_computation.28 | loop fusion | flops 6029312 | bytes 786432 | tf_op jit(solution)/shard_map/add | solution.py:211
  16.7 9.8 %sort.7 = s32[65536]{0:T(1024)S(1)} sort(s32[65536]{0:T(1024)} %fusion.5), dimensions={0}, to_apply=%region_0.1 | sort | flops 1048576 | bytes 524288 | tf_op jit(solution)/shard_map/sort | solution.py:212
  26.5 0.1 slice_reduce_fusion
  26.6 0.2 convert_reduce_fusion
  26.8 0.1 compare_convert_fusion
  26.9 0.1 reshape.54
  26.9 0.1 reduce_max.9.flag_ref
  27.1 0.1 fusion.31
  27.2 10.7 %counts.1 = (bf16[2048,3584]{1,0:T(8,128)(2,1)}, f32[2048,128]{1,0:T(8,128)}) custom-call(s32[112]{0:T(128)S(1)} %get-tuple-element.27.first_ref, s32[112]{0:T(128)S(1)} %get-tuple-element.26.last_ref, s32[8]{0:T(128)S(1)} %reduce_max.9.flag_ref, s32[512,128]{1,0:T(8,128)S(1)} %bitcast.8), custom_call_target="tpu_custom_call" | custom-call | tf_op jit(solution)/shard_map/counts/pallas_call | solution.py:224
  37.9 0.0 all-to-all-done
  37.9 0.0 copy-done.1
  37.9 0.0 copy-done.2
  37.9 0.0 copy-done.5
  37.9 12.1 %forward.1 = (bf16[2048,256]{1,0:T(8,128)(2,1)}, bf16[2048,256]{1,0:T(8,128)(2,1)}, bf16[2048,256]{1,0:T(8,128)(2,1)}, f32[512,256]{1,0:T(8,128)S(1)}) custom-call(bf16[2048,3584]{1,0:T(8,128)(2,1)} %get-tuple-element.12.adj_ref, f32[2048,128]{1,0:T(8,128)} %get-tuple-element.13.deg_ref, bf16[2048,256]{1,0:T(8,128)(2,1)S(1)} %copy-done, ...), custom_call_target="tpu_custom_call" | custom-call | tf_op jit(solution)/shard_map/forward/pallas_call | solution.py:251
  49.9 0.0 copy-start.3
  49.9 0.8 copy-done.3
  50.8 0.3 collective-permute-start
  51.1 0.0 copy-start.4
  51.1 5.8 %far.1 = bf16[1536,256]{1,0:T(8,128)(2,1)} custom-call(bf16[2048,3584]{1,0:T(8,128)(2,1)} %get-tuple-element.12.adj_ref, bf16[2048,256]{1,0:T(8,128)(2,1)} %get-tuple-element.15.dmsg_ref), custom_call_target="tpu_custom_call" | custom-call | tf_op jit(solution)/shard_map/far/pallas_call | solution.py:283
  56.9 0.0 collective-permute-done
  56.9 0.0 copy-done.4
  57.0 0.0 copy-start.7
  57.0 0.0 copy-start.8
  57.0 1.7 %collective-permute-start.1 = (f32[128,256]{1,0:T(8,128)S(1)}, f32[128,256]{1,0:T(8,128)S(1)}, u32[]{:S(2)}, u32[]{:S(2)}) collective-permute-start(f32[128,256]{1,0:T(8,128)S(1)} %constant_dynamic-slice_fusion), channel_id=1, source_target_pairs={{0,16},{8,24},{16,0},{24,8},{1,17},{9,25},{17,1},{25,9},{2,18},{10... | collective-permute-start | bytes 393224 | tf_op jit(solution)/shard_map/ppermute | solution.py:149
  58.8 4.0 %collective-permute-done.1 = f32[128,256]{1,0:T(8,128)S(1)} collective-permute-done((f32[128,256]{1,0:T(8,128)S(1)}, f32[128,256]{1,0:T(8,128)S(1)}, u32[]{:S(2)}, u32[]{:S(2)}) %collective-permute-start.1) | collective-permute-done | bytes 131104 | tf_op jit(solution)/shard_map/ppermute | solution.py:149
  62.8 1.8 %collective-permute-start.2 = (f32[128,256]{1,0:T(8,128)S(1)}, f32[128,256]{1,0:T(8,128)S(1)}, u32[]{:S(2)}, u32[]{:S(2)}) collective-permute-start(f32[128,256]{1,0:T(8,128)S(1)} %dynamic-slice_add_fusion.1), channel_id=1, source_target_pairs={{0,1},{1,0},{2,3},{3,2},{4,5},{5,4},{6,7},{7,6},{8,9},{9,8},{10,11... | collective-permute-start | bytes 393224 | tf_op jit(solution)/shard_map/ppermute | solution.py:157
  64.6 3.2 %collective-permute-done.2 = f32[128,256]{1,0:T(8,128)S(1)} collective-permute-done((f32[128,256]{1,0:T(8,128)S(1)}, f32[128,256]{1,0:T(8,128)S(1)}, u32[]{:S(2)}, u32[]{:S(2)}) %collective-permute-start.2) | collective-permute-done | bytes 131104 | tf_op jit(solution)/shard_map/ppermute | solution.py:157
  67.8 2.7 %collective-permute-start.3 = (f32[128,256]{1,0:T(8,128)S(1)}, f32[128,256]{1,0:T(8,128)S(1)}, u32[]{:S(2)}, u32[]{:S(2)}) collective-permute-start(f32[128,256]{1,0:T(8,128)S(1)} %add.138), channel_id=1, source_target_pairs={{0,2},{1,3},{2,0},{3,1},{4,6},{5,7},{6,4},{7,5},{8,10},{9,11},{10,... | collective-permute-start | bytes 393224 | tf_op jit(solution)/shard_map/ppermute | solution.py:157
  70.6 2.9 %collective-permute-done.3 = f32[128,256]{1,0:T(8,128)S(1)} collective-permute-done((f32[128,256]{1,0:T(8,128)S(1)}, f32[128,256]{1,0:T(8,128)S(1)}, u32[]{:S(2)}, u32[]{:S(2)}) %collective-permute-start.3) | collective-permute-done | bytes 131104 | tf_op jit(solution)/shard_map/ppermute | solution.py:157
  73.5 2.1 %collective-permute-start.4 = (f32[128,256]{1,0:T(8,128)S(1)}, f32[128,256]{1,0:T(8,128)S(1)}, u32[]{:S(2)}, u32[]{:S(2)}) collective-permute-start(f32[128,256]{1,0:T(8,128)S(1)} %add.139), channel_id=1, source_target_pairs={{0,4},{1,5},{2,6},{3,7},{4,0},{5,1},{6,2},{7,3},{8,12},{9,13},{10,... | collective-permute-start | bytes 393224 | tf_op jit(solution)/shard_map/ppermute | solution.py:157
  75.6 4.3 %all-to-all-start.1 = ((bf16[32,48,256]{2,1,0:T(8,128)(2,1)}), bf16[32,48,256]{2,1,0:T(8,128)(2,1)S(1)}, u32[]{:S(2)}, u32[]{:S(2)}) async-start(bf16[32,48,256]{2,1,0:T(8,128)(2,1)} %bitcast.3), calls=%async_computation.1 | async-start | bytes 1572864 | tf_op jit(solution)/shard_map/all_to_all | solution.py:296
  79.9 0.0 collective-permute-done.4
  79.9 2.1 %collective-permute-start.5 = (bf16[128,256]{1,0:T(8,128)(2,1)S(1)}, bf16[128,256]{1,0:T(8,128)(2,1)S(1)}, u32[]{:S(2)}, u32[]{:S(2)}) collective-permute-start(bf16[128,256]{1,0:T(8,128)(2,1)S(1)} %add_convert_fusion), channel_id=1, source_target_pairs={{0,16},{8,24},{16,0},{24,8},{1,17},{9,25},{17,1},{25,9},{2,18},{10... | collective-permute-start | bytes 196616 | tf_op jit(solution)/shard_map/ppermute | solution.py:161
  82.1 0.0 copy-done.7
  82.1 0.1 reshape.50
  82.1 0.0 copy-done.8
  82.2 6.7 %collective-permute-done.5 = bf16[128,256]{1,0:T(8,128)(2,1)S(1)} collective-permute-done((bf16[128,256]{1,0:T(8,128)(2,1)S(1)}, bf16[128,256]{1,0:T(8,128)(2,1)S(1)}, u32[]{:S(2)}, u32[]{:S(2)}) %collective-permute-start.5) | collective-permute-done | bytes 65568 | tf_op jit(solution)/shard_map/ppermute | solution.py:161
  88.9 0.1 collective-permute-start.6
  89.0 0.1 pad_add_fusion
  89.1 0.1 reshape.51.index_ref
  89.2 6.9 %own.1.base_ref = f32[2048,256]{1,0:T(8,128)S(1)} custom-call(bf16[2048,3584]{1,0:T(8,128)(2,1)} %get-tuple-element.12.adj_ref, bf16[2048,256]{1,0:T(8,128)(2,1)} %get-tuple-element.15.dmsg_ref, bf16[2048,256]{1,0:T(8,128)(2,1)} %get-tuple-element.16.g_ref, bf16[256,256]{1,0:T(8,128)(2,1)S(1)} %copy-done.2), custom_call_target="tpu_custom_call" | custom-call | tf_op jit(solution)/shard_map/own/pallas_call | solution.py:299
  96.1 0.0 collective-permute-done.6
  96.1 0.1 broadcast_select_fusion.1
  96.2 0.8 fusion.30
  97.0 4.8 %all-to-all-done.1 = bf16[32,48,256]{2,1,0:T(8,128)(2,1)S(1)} async-done(((bf16[32,48,256]{2,1,0:T(8,128)(2,1)}), bf16[32,48,256]{2,1,0:T(8,128)(2,1)S(1)}, u32[]{:S(2)}, u32[]{:S(2)}) %all-to-all-start.1) | async-done | bytes 786464 | tf_op jit(solution)/shard_map/all_to_all | solution.py:296
  101.9 4.5 %finish.1 = bf16[2048,256]{1,0:T(8,128)(2,1)} custom-call(s32[1,1536]{1,0:T(1,128)S(1)} %reshape.51.index_ref, f32[2048,256]{1,0:T(8,128)S(1)} %own.1.base_ref, bf16[1536,256]{1,0:T(8,128)(2,1)S(1)} %bitcast.6), custom_call_target="tpu_custom_call" | custom-call | tf_op jit(solution)/shard_map/finish/pallas_call | solution.py:317
  (14 shorter events, 0.2 us)
Async XLA Ops:
  0.6 4.4 %copy-start = (bf16[2048,256]{1,0:T(8,128)(2,1)S(1)}, bf16[2048,256]{1,0:T(8,128)(2,1)}, u32[]{:S(2)}) copy-start(bf16[2048,256]{1,0:T(8,128)(2,1)} %feats_ref.1) | copy-start | bytes 3145732
  5.7 8.3 %copy-start.6 = (s32[65536]{0:T(1024)S(1)}, s32[65536]{0:T(1024)}, u32[]{:S(2)}) copy-start(s32[65536]{0:T(1024)} %param.15) | copy-start | bytes 786436
  6.7 31.2 %copy-start.1 = (bf16[2048,256]{1,0:T(8,128)(2,1)S(1)}, bf16[2048,256]{1,0:T(8,128)(2,1)}, u32[]{:S(2)}) copy-start(bf16[2048,256]{1,0:T(8,128)(2,1)} %cot_ref.1) | copy-start | bytes 3145732
  6.7 31.2 %copy-start.2 = (bf16[256,256]{1,0:T(8,128)(2,1)S(1)}, bf16[256,256]{1,0:T(8,128)(2,1)}, u32[]{:S(2)}) copy-start(bf16[256,256]{1,0:T(8,128)(2,1)} %ws_ref.3) | copy-start | bytes 393220
  6.7 31.2 %copy-start.5 = (bf16[256,256]{1,0:T(8,128)(2,1)S(1)}, bf16[256,256]{1,0:T(8,128)(2,1)}, u32[]{:S(2)}) copy-start(bf16[256,256]{1,0:T(8,128)(2,1)} %wn_ref.1) | copy-start | bytes 393220
  6.7 31.2 %all-to-all-start = ((bf16[32,48,256]{2,1,0:T(8,128)(2,1)}), bf16[32,48,256]{2,1,0:T(8,128)(2,1)S(1)}, u32[]{:S(2)}, u32[]{:S(2)}) async-start(bf16[32,48,256]{2,1,0:T(8,128)(2,1)} %pad_maximum_fusion), calls=%async_computation | async-start | bytes 1572864 | tf_op jit(solution)/shard_map/all_to_all | solution.py:202
  49.9 0.8 copy-start.3
  50.8 6.2 %collective-permute-start = (f32[256,256]{1,0:T(8,128)S(1)}, f32[256,256]{1,0:T(8,128)S(1)}, u32[]{:S(2)}, u32[]{:S(2)}) collective-permute-start(f32[256,256]{1,0:T(8,128)S(1)} %constant_dynamic-slice_fusion.1), channel_id=1, source_target_pairs={{0,8},{8,0},{16,24},{24,16},{1,9},{9,1},{17,25},{25,17},{2,10},{10... | collective-permute-start | bytes 786440 | tf_op jit(solution)/shard_map/ppermute | solution.py:149
  51.1 5.9 %copy-start.4 = (f32[512,256]{1,0:T(8,128)S(1)}, f32[512,256]{1,0:T(8,128)}, u32[]{:S(2)}) copy-start(f32[512,256]{1,0:T(8,128)} %copy-done.3) | copy-start | bytes 1572868
  57.0 25.1 %copy-start.7 = (s32[512]{0:T(512)S(1)}, s32[512]{0:T(512)}, u32[]{:S(2)}) copy-start(s32[512]{0:T(512)} %param.13) | copy-start | bytes 6148
  57.0 25.1 %copy-start.8 = (s32[32]{0:T(128)S(1)}, s32[32]{0:T(128)}, u32[]{:S(2)}) copy-start(s32[32]{0:T(128)} %param.12) | copy-start | bytes 388
  57.0 5.8 %collective-permute-start.1 = (f32[128,256]{1,0:T(8,128)S(1)}, f32[128,256]{1,0:T(8,128)S(1)}, u32[]{:S(2)}, u32[]{:S(2)}) collective-permute-start(f32[128,256]{1,0:T(8,128)S(1)} %constant_dynamic-slice_fusion), channel_id=1, source_target_pairs={{0,16},{8,24},{16,0},{24,8},{1,17},{9,25},{17,1},{25,9},{2,18},{10... | collective-permute-start | bytes 393224 | tf_op jit(solution)/shard_map/ppermute | solution.py:149
  62.8 5.0 %collective-permute-start.2 = (f32[128,256]{1,0:T(8,128)S(1)}, f32[128,256]{1,0:T(8,128)S(1)}, u32[]{:S(2)}, u32[]{:S(2)}) collective-permute-start(f32[128,256]{1,0:T(8,128)S(1)} %dynamic-slice_add_fusion.1), channel_id=1, source_target_pairs={{0,1},{1,0},{2,3},{3,2},{4,5},{5,4},{6,7},{7,6},{8,9},{9,8},{10,11... | collective-permute-start | bytes 393224 | tf_op jit(solution)/shard_map/ppermute | solution.py:157
  67.8 5.7 %collective-permute-start.3 = (f32[128,256]{1,0:T(8,128)S(1)}, f32[128,256]{1,0:T(8,128)S(1)}, u32[]{:S(2)}, u32[]{:S(2)}) collective-permute-start(f32[128,256]{1,0:T(8,128)S(1)} %add.138), channel_id=1, source_target_pairs={{0,2},{1,3},{2,0},{3,1},{4,6},{5,7},{6,4},{7,5},{8,10},{9,11},{10,... | collective-permute-start | bytes 393224 | tf_op jit(solution)/shard_map/ppermute | solution.py:157
  73.5 6.4 %collective-permute-start.4 = (f32[128,256]{1,0:T(8,128)S(1)}, f32[128,256]{1,0:T(8,128)S(1)}, u32[]{:S(2)}, u32[]{:S(2)}) collective-permute-start(f32[128,256]{1,0:T(8,128)S(1)} %add.139), channel_id=1, source_target_pairs={{0,4},{1,5},{2,6},{3,7},{4,0},{5,1},{6,2},{7,3},{8,12},{9,13},{10,... | collective-permute-start | bytes 393224 | tf_op jit(solution)/shard_map/ppermute | solution.py:157
  75.6 26.3 %all-to-all-start.1 = ((bf16[32,48,256]{2,1,0:T(8,128)(2,1)}), bf16[32,48,256]{2,1,0:T(8,128)(2,1)S(1)}, u32[]{:S(2)}, u32[]{:S(2)}) async-start(bf16[32,48,256]{2,1,0:T(8,128)(2,1)} %bitcast.3), calls=%async_computation.1 | async-start | bytes 1572864 | tf_op jit(solution)/shard_map/all_to_all | solution.py:296
  79.9 9.0 %collective-permute-start.5 = (bf16[128,256]{1,0:T(8,128)(2,1)S(1)}, bf16[128,256]{1,0:T(8,128)(2,1)S(1)}, u32[]{:S(2)}, u32[]{:S(2)}) collective-permute-start(bf16[128,256]{1,0:T(8,128)(2,1)S(1)} %add_convert_fusion), channel_id=1, source_target_pairs={{0,16},{8,24},{16,0},{24,8},{1,17},{9,25},{17,1},{25,9},{2,18},{10... | collective-permute-start | bytes 196616 | tf_op jit(solution)/shard_map/ppermute | solution.py:161
  88.9 7.1 %collective-permute-start.6 = (bf16[256,256]{1,0:T(8,128)(2,1)S(1)}, bf16[256,256]{1,0:T(8,128)(2,1)S(1)}, u32[]{:S(2)}, u32[]{:S(2)}) collective-permute-start(bf16[256,256]{1,0:T(8,128)(2,1)S(1)} %pad_maximum_fusion.1), channel_id=1, source_target_pairs={{0,8},{8,0},{16,24},{24,16},{1,9},{9,1},{17,25},{25,17},{2,10},{10... | collective-permute-start | bytes 393224 | tf_op jit(solution)/shard_map/ppermute | solution.py:161

commit v3 on v2

--- a/solution.py
+++ b/solution.py
@@ -86,12 +86,23 @@
         lax.fori_loop(0, all_tiles, rest, 0)
 
 
-def forward_kernel(adj_ref, deg_ref, feats_ref, remote_ref, ws_ref, wn_ref, cot_ref,
-                   out_ref, g_ref, dmsg_ref, grads_ref):
+def forward_kernel(core_ref, adj_ref, deg_ref, feats_ref, remote_ref, ws_ref, wn_ref, cot_ref,
+                   out_ref, g_ref, dmsg_ref, grads_ref, table_ref, *, chunk):
     block = pl.program_id(0)
+    pairs = remote_ref.shape[0] // chunk // 2
+
+    @pl.when(block == 0)
+    def _():
+        for half in range(2):
+            for pair in range(pairs):
+                start = (2 * pair + (core_ref[0] ^ half)) * chunk
+                table_ref[pl.ds((half * pairs + pair) * chunk, chunk), :] = remote_ref[
+                    pl.ds(pl.multiple_of(start, 16), chunk), :
+                ]
+
     rows, width = out_ref.shape
     own = feats_ref.shape[0]
-    total = mm(adj_ref[:, :own], feats_ref[...]) + mm(adj_ref[:, own:], remote_ref[...])
+    total = mm(adj_ref[:, :own], feats_ref[...]) + mm(adj_ref[:, own:], table_ref[...])
     degree = jnp.sum(deg_ref[...], axis=1, keepdims=True)
     inverse = 1.0 / jnp.maximum(degree, 1.0)
     mean = (total * inverse).astype(jnp.bfloat16)
@@ -112,11 +123,13 @@
     grads_ref[width:, :] += outer_tn(mean, g)
 
 
-def far_kernel(adj_ref, dmsg_ref, back_ref):
+def far_kernel(adj_ref, dmsg_ref, *refs):
+    back_ref = refs[-1]
     back_ref[...] = outer_tn(adj_ref[...], dmsg_ref[...]).astype(jnp.bfloat16)
 
 
-def own_kernel(adj_ref, dmsg_ref, g_ref, ws_ref, base_ref):
+def own_kernel(adj_ref, dmsg_ref, g_ref, ws_ref, *refs):
+    base_ref = refs[-1]
     base_ref[...] = outer_tn(adj_ref[...], dmsg_ref[...]) + outer_nt(g_ref[...], ws_ref[...])
 
 
@@ -134,41 +147,44 @@
     out_ref[...] = (base_ref[...] + mm(pick, back_ref[...])).astype(jnp.bfloat16)
 
 
-def all_reduce(parts, gate):
-    dom = lax.axis_size("dom")
-    sub = lax.axis_size("sub")
-    at = lax.axis_index("dom")
-    steps = []
-    stride = 1
-    while stride < dom:
-        half = parts.shape[0] // 2
-        bit = (at // stride) % 2
-        pairs = [(i, i ^ stride) for i in range(dom)]
-        sent = lax.dynamic_slice_in_dim(parts, (1 - bit) * half, half, 0)
-        kept = lax.dynamic_slice_in_dim(parts, bit * half, half, 0)
-        came = lax.ppermute(sent, "dom", pairs)
-        if stride == 1:
-            came, gate = lax.optimization_barrier((came, gate))
-        parts = kept + came
-        steps.append((bit, pairs))
-        stride *= 2
-    stride = 1
-    while stride < sub:
-        parts = parts + lax.ppermute(parts, "sub", [(i, i ^ stride) for i in range(sub)])
-        stride *= 2
-    parts = parts.astype(jnp.bfloat16)
-    for bit, pairs in reversed(steps):
-        other = lax.ppermute(parts, "dom", pairs)
-        low = jnp.where(bit == 0, parts, other)
-        high = jnp.where(bit == 0, other, parts)
-        parts = jnp.concatenate([low, high], axis=0)
-    return parts.astype(jnp.float32), gate
-
-
-def call(kernel, grid, in_specs, out_specs, out_shape, name, vmem):
+def gather_kernel(hub_ref, send_ref, feats_ref, out_ref, wide_ref, hubs_ref, sends_ref):
+    hub_dev = hubs_ref.shape[0]
+    count = sends_ref.shape[0]
+    devices = (out_ref.shape[0] - count) // hub_dev
+    cap = count // devices
+    pack = hub_dev + cap
+    wide_ref[...] = feats_ref[...].astype(jnp.float32)
+
+    def hub(i, carry):
+        hubs_ref[pl.ds(i, 1), :] = wide_ref[pl.ds(hub_ref[i], 1), :]
+        return carry
+
+    def send(i, carry):
+        sends_ref[pl.ds(i, 1), :] = wide_ref[pl.ds(send_ref[i], 1), :]
+        return carry
+
+    lax.fori_loop(0, hub_dev, hub, 0, unroll=8)
+    lax.fori_loop(0, count, send, 0, unroll=16)
+    hubs = hubs_ref[...].astype(jnp.bfloat16)
+
+    def place(p, carry):
+        out_ref[pl.ds(pl.multiple_of(p * pack, 16), hub_dev), :] = hubs
+        halo = sends_ref[pl.ds(pl.multiple_of(p * cap, 16), cap), :].astype(jnp.bfloat16)
+        out_ref[pl.ds(pl.multiple_of(p * pack + hub_dev, 16), cap), :] = halo
+        return carry
+
+    lax.fori_loop(0, devices, place, 0, unroll=4)
+
+
+def tie(*arrays):
+    return lax.optimization_barrier(arrays)
+
+
+def call(kernel, grid, in_specs, out_specs, out_shape, name, vmem, aliases=None):
     return pl.pallas_call(
         kernel,
         name=name,
+        input_output_aliases=aliases or {},
         grid=grid,
         in_specs=in_specs,
         out_specs=out_specs,
@@ -196,19 +212,48 @@
     bf16 = jnp.bfloat16
 
     send_table = send_rows.reshape(devices, cap)
-    hub_out = jnp.broadcast_to(feats[hub_rows][None], (devices, hub_dev, width))
-    halo_out = feats[send_rows].reshape(devices, cap, width)
-    outgoing = jnp.concatenate([hub_out, halo_out], axis=1)
+    outgoing = pl.pallas_call(
+        gather_kernel,
+        name="gather",
+        out_shape=jax.ShapeDtypeStruct((far, width), bf16),
+        grid_spec=pltpu.PrefetchScalarGridSpec(
+            num_scalar_prefetch=2,
+            grid=(1,),
+            in_specs=[pl.BlockSpec((vcount, width), lambda b, *_: (0, 0))],
+            out_specs=pl.BlockSpec((far, width), lambda b, *_: (0, 0)),
+            scratch_shapes=[
+                pltpu.VMEM((vcount, width), f32),
+                pltpu.VMEM((hub_dev, width), f32),
+                pltpu.VMEM((devices * cap, width), f32),
+            ],
+        ),
+        compiler_params=pltpu.CompilerParams(
+            dimension_semantics=("arbitrary",),
+            vmem_limit_bytes=(4 << 20) + width * (8 * vcount + 8 * far),
+        ),
+    )(
+        hub_rows,
+        send_rows,
+        pltpu.with_memory_space_constraint(feats, pltpu.HBM),
+    ).reshape(devices, pack, width)
     remote = lax.all_to_all(outgoing, AXES, split_axis=0, concat_axis=0, tiled=True)
     remote = remote.reshape(far, width)
 
     hub_at = edge_src - vcount
     halo_at = hub_at - devices * hub_dev
-    hub_slot = vcount + (hub_at // hub_dev) * pack + hub_at % hub_dev
-    halo_slot = vcount + (halo_at // cap) * pack + hub_dev + halo_at % cap
+    dom = lax.axis_size("dom")
+    sub = lax.axis_size("sub")
+    core = lax.axis_index("dom") % 2
+
+    def place(device):
+        d = lax.div(device, sub)
+        return (((d ^ core) & 1) * (dom // 2) + (d >> 1)) * sub + lax.rem(device, sub)
+
+    hub_slot = vcount + place(lax.div(hub_at, hub_dev)) * pack + lax.rem(hub_at, hub_dev)
+    halo_slot = vcount + place(lax.div(halo_at, cap)) * pack + hub_dev + lax.rem(halo_at, cap)
     slot = jnp.where(hub_at < 0, edge_src, jnp.where(halo_at < 0, hub_slot, halo_slot))
-    tile_id = (edge_dst // T) * all_tiles + slot // T
-    key = (tile_id * T + edge_dst % T) * T + slot % T
+    tile_id = (edge_dst >> 8) * all_tiles + (slot >> 8)
+    key = (tile_id << 16) | ((edge_dst & 255) << 8) | (slot & 255)
     keys = lax.sort(key, is_stable=False).reshape(key_rows, LANES)
     heads = keys[:, 0]
     limits = jnp.arange(tiles + 1, dtype=jnp.int32) * (T * T)
@@ -245,57 +290,99 @@
 
     adj = pltpu.with_memory_space_constraint(adj, pltpu.HBM)
     deg = pltpu.with_memory_space_constraint(deg, pltpu.HBM)
-    whole = lambda b: (0, 0)
-    by_row = lambda b: (b, 0)
+    whole = lambda b, *_: (0, 0)
+    by_row = lambda b, *_: (b, 0)
     rows = min(2 * T, vcount)
-    layer_out, g, dmsg, parts = call(
-        forward_kernel,
-        (vcount // rows,),
-        [
-            pl.BlockSpec((rows, slots), by_row),
-            pl.BlockSpec((rows, LANES), by_row),
-            pl.BlockSpec((vcount, width), whole),
-            pl.BlockSpec((far, width), whole),
-            pl.BlockSpec((width, width), whole),
-            pl.BlockSpec((width, width), whole),
-            pl.BlockSpec((rows, width), by_row),
-        ],
-        [
-            pl.BlockSpec((rows, width), by_row),
-            pl.BlockSpec((rows, width), by_row),
-            pl.BlockSpec((rows, width), by_row),
-            pl.BlockSpec((2 * width, width), whole),
-        ],
-        (
+    layer_out, g, dmsg, parts = pl.pallas_call(
+        functools.partial(forward_kernel, chunk=sub * pack),
+        name="forward",
+        grid_spec=pltpu.PrefetchScalarGridSpec(
+            num_scalar_prefetch=1,
+            grid=(vcount // rows,),
+            in_specs=[
+                pl.BlockSpec((rows, slots), by_row),
+                pl.BlockSpec((rows, LANES), by_row),
+                pl.BlockSpec((vcount, width), whole),
+                pl.BlockSpec((far, width), whole),
+                pl.BlockSpec((width, width), whole),
+                pl.BlockSpec((width, width), whole),
+                pl.BlockSpec((rows, width), by_row),
+            ],
+            out_specs=[
+                pl.BlockSpec((rows, width), by_row),
+                pl.BlockSpec((rows, width), by_row),
+                pl.BlockSpec((rows, width), by_row),
+                pl.BlockSpec((2 * width, width), whole),
+            ],
+            scratch_shapes=[pltpu.VMEM((far, width), bf16)],
+        ),
+        out_shape=(
             pltpu.HBM((vcount, width), bf16),
             pltpu.HBM((vcount, width), bf16),
             pltpu.HBM((vcount, width), bf16),
             jax.ShapeDtypeStruct((2 * width, width), f32),
         ),
-        "forward",
-        (8 << 20) + 4 * rows * slots + 4 * slots * width,
-    )(adj, deg, feats, remote, w_self, w_neigh, cotangent)
+        compiler_params=pltpu.CompilerParams(
+            dimension_semantics=("arbitrary",),
+            vmem_limit_bytes=(8 << 20) + 4 * rows * slots + 6 * slots * width,
+        ),
+    )(
+        jnp.reshape(core, (1,)).astype(jnp.int32),
+        adj,
+        deg,
+        feats,
+        remote,
+        w_self,
+        w_neigh,
+        pltpu.with_memory_space_constraint(cotangent, pltpu.HBM),
+    )
 
     g = pltpu.with_memory_space_constraint(g, pltpu.HBM)
     dmsg = pltpu.with_memory_space_constraint(dmsg, pltpu.HBM)
+    half = devices // 2
+    twin = [(i, i ^ 1) for i in range(dom)]
+    groups = [
+        [d * sub + i for d in range(c, dom, 2) for i in range(sub)] for c in range(2)
+    ]
+
+    def exchange(x):
+        return lax.all_to_all(
+            x, AXES, split_axis=0, concat_axis=0, axis_index_groups=groups, tiled=True
+        )
+
+    def far_part(start, dmsg):
+        return call(
+            far_kernel,
+            (far // 2 // T,),
+            [
+                pl.BlockSpec((vcount, T), lambda j: (0, j + start // T)),
+                pl.BlockSpec((vcount, width), whole),
+            ],
+            pl.BlockSpec((T, width), by_row),
+            jax.ShapeDtypeStruct((far // 2, width), bf16),
+            "far",
+            16 << 20,
+        )(adj, dmsg)
+
+    sent = lax.dynamic_slice_in_dim(parts, (1 - core) * width, width, 0)
+    kept = lax.dynamic_slice_in_dim(parts, core * width, width, 0)
+    came = lax.ppermute(sent, "dom", twin)
+    given = far_part(vcount + far // 2, dmsg)
+    got = lax.ppermute(given, "dom", twin)
+    dmsg, given = tie(dmsg, given)
+    kept_slots = far_part(vcount, dmsg)
+    came, kept_slots = tie(came, kept_slots)
+    share = width // half
+    piece = (kept + came).astype(bf16).reshape(half, share, width)
+    kept_slots = kept_slots.reshape(half, pack, width)
+    got = got.reshape(half, pack, width)
+    hub_sum = kept_slots[:, :hub_dev].astype(f32) + got[:, :hub_dev].astype(f32)
+    payload = jnp.concatenate(
+        [hub_sum.astype(bf16), kept_slots[:, hub_dev:], got[:, hub_dev:], piece], axis=1
+    )
+    bundle = payload.shape[1]
+    returned = exchange(payload)
     cols = 2 * T
-    skip = vcount // cols
-    back = call(
-        far_kernel,
-        (far // cols,),
-        [
-            pl.BlockSpec((vcount, cols), lambda j: (0, j + skip)),
-            pl.BlockSpec((vcount, width), whole),
-        ],
-        pl.BlockSpec((cols, width), by_row),
-        jax.ShapeDtypeStruct((far, width), bf16),
-        "far",
-        16 << 20,
-    )(adj, dmsg)
-    grads, back = all_reduce(parts, back)
-    returned = lax.all_to_all(
-        back.reshape(devices, pack, width), AXES, split_axis=0, concat_axis=0, tiled=True
-    ).reshape(far, width)
     base = call(
         own_kernel,
         (vcount // cols,),
@@ -311,23 +398,39 @@
         16 << 20,
     )(adj, dmsg, g, w_self)
 
+    mine = jnp.sum(returned[:, bundle - share :].astype(f32), axis=0).astype(bf16)
+    mine, base = tie(mine, base)
+    mine = exchange(jnp.broadcast_to(mine[None], (half, share, width))).reshape(width, width)
+    table = send_rows.reshape(dom // 2, 2, sub, cap)
+    near = lax.dynamic_index_in_dim(table, core, 1, keepdims=False).reshape(half, cap)
+    away = lax.dynamic_index_in_dim(table, 1 - core, 1, keepdims=False).reshape(half, cap)
     index = jnp.concatenate(
-        [jnp.broadcast_to(hub_rows[None], (devices, hub_dev)), send_table], axis=1
-    ).reshape(1, far)
+        [
+            jnp.broadcast_to(hub_rows[None], (half, hub_dev)),
+            near,
+            away,
+            jnp.full((half, share), -1, jnp.int32),
+        ],
+        axis=1,
+    ).reshape(1, half * bundle)
     grad_feats = call(
         finish_kernel,
-        (own_tiles,),
+        (vcount // rows,),
         [
-            pl.BlockSpec((1, far), whole),
-            pl.BlockSpec((T, width), by_row),
-            pl.BlockSpec((far, width), whole),
+            pl.BlockSpec((1, half * bundle), whole),
+            pl.BlockSpec((rows, width), by_row),
+            pl.BlockSpec((half * bundle, width), whole),
         ],
-        pl.BlockSpec((T, width), by_row),
+        pl.BlockSpec((rows, width), by_row),
         jax.ShapeDtypeStruct((vcount, width), bf16),
         "finish",
         (8 << 20) + 8 * far * width,
-    )(index, base, returned)
-    return (layer_out, grad_feats, grads[:width], grads[width:])
+    )(index, base, returned.reshape(half * bundle, width))
+    mine, grad_feats = tie(mine, grad_feats)
+    other = lax.ppermute(mine, "dom", twin)
+    grad_self = jnp.where(core == 0, mine, other).astype(f32)
+    grad_neigh = jnp.where(core == 0, other, mine).astype(f32)
+    return (layer_out, grad_feats, grad_self, grad_neigh)
 
 
 def solution(mesh):

time: 107 us -> 96.2 us (0.90)
  Pallas kernels: 40 us -> 45.2 us
  starting transfers between devices: 22.4 us -> 17.2 us
  waiting for transfers between devices: 21.8 us -> 18 us
  other arithmetic: 15.6 us -> 11.8 us
  local copies, waits for them, and re-layouts: 5.68 us -> 2.55 us
    ppermute x7 -> x3, waiting for transfers between devices: 16.9 us -> 1.35 us  [the longest x1 1.35 us: body(): other = lax.ppermute(mine, 'dom', twin)]
    all_to_all x1 -> x2, waiting for transfers between devices: 4.85 us -> 15.6 us  [exchange(): lax.all_to_all(x, AXES, split_axis=0, concat_axis=0, axis_index_groups=gr...]
    ppermute x7 -> x3, starting transfers between devices: 10.9 us -> 0.62 us  [the longest x1 0.55 us: body(): got = lax.ppermute(given, 'dom', twin)]
    pallas_call x3 -> x5, Pallas kernels: 22.4 us -> 27.6 us  [the longest x1 12.2 us: body(): pl.pallas_call(functools.partial(forward_kernel, chunk=sub * pack), name=...]
    all_to_all x1 -> x2, starting transfers between devices: 4.28 us -> 9.27 us  [exchange(): lax.all_to_all(x, AXES, split_axis=0, concat_axis=0, axis_index_groups=gr...]
    gather x2 -> x0, local copies, waits for them, and re-layouts: 3.55 us -> none  [the longest x1 2.92 us: body(): halo_out = feats[send_rows].reshape(devices, cap, width)]
    add x5 -> x0, other arithmetic: 2.76 us -> none  [the longest x1 2.68 us: body(): key = (tile_id * T + edge_dst % T) * T + slot % T]
    select_n x4 -> x0, other arithmetic: 1.5 us -> none  [the longest x1 0.77 us: body(): halo_out = feats[send_rows].reshape(devices, cap, width)]
  transfers between devices with their start and end apart: 9 -> 6, of which waited for: 5 -> 4; matrix products, arithmetic and copies ran while one was open for 13% -> 11% of each run, Pallas kernels for 22% -> 29%
where the time goes in v3:
time: 96.2 us; the launch traced here: 95.6 us
  Pallas kernels  45.2 us (47%)
  waiting for transfers between devices  18 us (19%)
  starting transfers between devices  17.2 us (18%)
  other arithmetic  11.8 us (12%)
  local copies, waits for them, and re-layouts  2.55 us (3%)
    all_to_all x2, waiting for transfers between devices, exchange(): lax.all_to_all(x, AXES, split_axis=0, concat_axis=0, axis_index_groups=gr...  15.6 us
    pallas_call x1, Pallas kernels, body(): pl.pallas_call(functools.partial(forward_kernel, chunk=sub * pack), name=...  12.2 us
    pallas_call x1, Pallas kernels, body(): pl.pallas_call(functools.partial(counts_kernel, all_tiles=all_tiles, wind...  10.7 us
    all_to_all x2, starting transfers between devices, exchange(): lax.all_to_all(x, AXES, split_axis=0, concat_axis=0, axis_index_groups=gr...  9.27 us
    sort x1, other arithmetic, body(): keys = lax.sort(key, is_stable=False).reshape(key_rows, LANES)  8.79 us
    pallas_call x2, Pallas kernels, far_part(): call(far_kernel, (far // 2 // T,), [pl.BlockSpec((vcount, T), lambda j: (...  7.57 us
    all_to_all x1, starting transfers between devices, body(): lax.all_to_all(outgoing, AXES, split_axis=0, concat_axis=0, tiled=True)  7.3 us
    pallas_call x1, Pallas kernels, body(): call(own_kernel, (vcount // cols,), [pl.BlockSpec((vcount, cols), lambda...  6.89 us
  transfers between devices with their start and end apart: 6, of which 4 were waited for; matrix products, arithmetic and copies ran while one was open for 11% of the time, Pallas kernels for 29%

profile of v3, /device:TPU:0, one launch (start us, length us, event | category | flops | bytes accessed | tf_op | source)
XLA Modules:
  0.0 95.6 jit_solution(10597965819943402566)
XLA Ops:
  0.6 0.0 copy-start.3
  0.6 0.7 copy-done.3
  1.3 0.0 copy-start.5
  1.3 0.7 copy-done.5
  2.0 0.0 copy-start.7
  2.0 0.0 copy-start.8
  2.0 4.8 %gather.1 = bf16[1536,256]{1,0:T(8,128)(2,1)} custom-call(s32[32]{0:T(128)S(1)} %copy-done.5, s32[512]{0:T(512)S(1)} %copy-done.3, bf16[2048,256]{1,0:T(8,128)(2,1)} %feats_ref.3), custom_call_target="tpu_custom_call" | custom-call | tf_op jit(solution)/shard_map/gather/pallas_call | solution.py:215
  6.8 7.3 %all-to-all-start = ((bf16[32,48,256]{2,1,0:T(8,128)(2,1)}), bf16[32,48,256]{2,1,0:T(8,128)(2,1)S(1)}, u32[]{:S(2)}, u32[]{:S(2)}) async-start(bf16[32,48,256]{2,1,0:T(8,128)(2,1)} %bitcast.2), calls=%async_computation | async-start | bytes 1572864 | tf_op jit(solution)/shard_map/all_to_all | solution.py:239
  14.1 0.0 copy-start
  14.1 0.0 copy-start.1
  14.1 0.0 copy-start.2
  14.2 0.0 copy-done.7
  14.2 0.0 copy-done.8
  14.2 0.6 and_or_fusion
  14.8 8.8 %sort.7 = s32[65536]{0:T(1024)S(1)} sort(s32[65536]{0:T(1024)S(1)} %and_or_fusion), dimensions={0}, to_apply=%region_0.1 | sort | flops 1048576 | bytes 524288 | tf_op jit(solution)/shard_map/sort | solution.py:257
  23.6 0.1 slice_reduce_fusion
  23.7 0.2 convert_reduce_fusion
  23.9 0.1 compare_convert_fusion
  24.0 0.1 reshape.80
  24.1 0.1 reduce_max.9.flag_ref
  24.2 0.1 fusion.14
  24.3 10.7 %counts.1 = (bf16[2048,3584]{1,0:T(8,128)(2,1)}, f32[2048,128]{1,0:T(8,128)}) custom-call(s32[112]{0:T(128)S(1)} %get-tuple-element.35.first_ref, s32[112]{0:T(128)S(1)} %get-tuple-element.34.last_ref, s32[8]{0:T(128)S(1)} %reduce_max.9.flag_ref, s32[512,128]{1,0:T(8,128)S(1)} %bitcast.16), custom_call_target="tpu_custom_call" | custom-call | tf_op jit(solution)/shard_map/counts/pallas_call | solution.py:269
  35.0 1.1 %all-to-all-done = bf16[32,48,256]{2,1,0:T(8,128)(2,1)S(1)} async-done(((bf16[32,48,256]{2,1,0:T(8,128)(2,1)}), bf16[32,48,256]{2,1,0:T(8,128)(2,1)S(1)}, u32[]{:S(2)}, u32[]{:S(2)}) %all-to-all-start) | async-done | bytes 786464 | tf_op jit(solution)/shard_map/all_to_all | solution.py:239
  36.1 0.0 copy-done
  36.1 0.0 copy-done.1
  36.1 0.0 copy-done.2
  36.1 12.2 %forward.1 = (bf16[2048,256]{1,0:T(8,128)(2,1)}, bf16[2048,256]{1,0:T(8,128)(2,1)}, bf16[2048,256]{1,0:T(8,128)(2,1)}, f32[512,256]{1,0:T(8,128)S(1)}) custom-call(s32[1]{0:T(128)} %bitcast.core_ref, bf16[2048,3584]{1,0:T(8,128)(2,1)} %get-tuple-element.17.adj_ref, f32[2048,128]{1,0:T(8,128)} %get-tuple-element.18.deg_ref, bf16[2048,256]{1,0:T(8,128)(2,1)S(1)} %copy-done, ...), custom_call_target="tpu_custom_call" | custom-call | tf_op jit(solution)/shard_map/forward/pallas_call | solution.py:296
  48.3 0.1 collective-permute-start
  48.4 3.8 %far.2 = bf16[768,256]{1,0:T(8,128)(2,1)S(1)} custom-call(bf16[2048,3584]{1,0:T(8,128)(2,1)} %get-tuple-element.17.adj_ref, bf16[2048,256]{1,0:T(8,128)(2,1)} %get-tuple-element.22.dmsg_ref), custom_call_target="tpu_custom_call" | custom-call | tf_op jit(solution)/shard_map/far/pallas_call | solution.py:354
  52.2 0.6 collective-permute-start.1
  52.8 3.8 %far.3 = bf16[768,256]{1,0:T(8,128)(2,1)S(1)} custom-call(bf16[2048,3584]{1,0:T(8,128)(2,1)} %get-tuple-element.17.adj_ref, bf16[2048,256]{1,0:T(8,128)(2,1)} %get-tuple-element.22.dmsg_ref), custom_call_target="tpu_custom_call" | custom-call | tf_op jit(solution)/shard_map/far/pallas_call | solution.py:354
  56.6 0.0 collective-permute-done
  56.6 0.0 collective-permute-done.1
  56.7 0.1 add_convert_fusion
  56.7 0.0 copy-start.4
  56.7 0.9 pad_maximum_fusion
  57.6 5.8 %all-to-all-start.1 = ((bf16[16,80,256]{2,1,0:T(8,128)(2,1)}), bf16[16,80,256]{2,1,0:T(8,128)(2,1)S(1)}, u32[]{:S(2)}, u32[]{:S(2)}) async-start(bf16[16,80,256]{2,1,0:T(8,128)(2,1)} %pad_maximum_fusion), calls=%async_computation.1 | async-start | bytes 1310720 | tf_op jit(solution)/shard_map/all_to_all | solution.py:349
  63.4 0.0 copy-done.4
  63.4 0.1 reshape.75
  63.5 0.0 copy-start.6
  63.5 6.9 %own.1.base_ref = f32[2048,256]{1,0:T(8,128)S(1)} custom-call(bf16[2048,3584]{1,0:T(8,128)(2,1)} %get-tuple-element.17.adj_ref, bf16[2048,256]{1,0:T(8,128)(2,1)} %get-tuple-element.22.dmsg_ref, bf16[2048,256]{1,0:T(8,128)(2,1)} %get-tuple-element.25.g_ref, bf16[256,256]{1,0:T(8,128)(2,1)S(1)} %copy-done.1), custom_call_target="tpu_custom_call" | custom-call | tf_op jit(solution)/shard_map/own/pallas_call | solution.py:386
  70.4 11.1 %all-to-all-done.1 = bf16[16,80,256]{2,1,0:T(8,128)(2,1)S(1)} async-done(((bf16[16,80,256]{2,1,0:T(8,128)(2,1)}), bf16[16,80,256]{2,1,0:T(8,128)(2,1)S(1)}, u32[]{:S(2)}, u32[]{:S(2)}) %all-to-all-start.1) | async-done | bytes 655392 | tf_op jit(solution)/shard_map/all_to_all | solution.py:349
  81.5 0.7 broadcast_in_dim.6
  82.1 3.5 %all-to-all-start.2 = ((bf16[16,16,256]{2,1,0:T(8,128)(2,1)}), bf16[16,16,256]{2,1,0:T(8,128)(2,1)S(1)}, u32[]{:S(2)}, u32[]{:S(2)}) async-start(bf16[16,16,256]{2,1,0:T(8,128)(2,1)} %broadcast_in_dim.6), calls=%async_computation.2 | async-start | bytes 262144 | tf_op jit(solution)/shard_map/all_to_all | solution.py:349
  85.7 0.0 copy-done.6
  85.7 0.1 pad.3.clone
  85.8 0.1 add_add_fusion
  85.8 0.1 reshape.78.index_ref
  85.9 3.0 %finish.1 = bf16[2048,256]{1,0:T(8,128)(2,1)} custom-call(s32[1,1280]{1,0:T(1,128)S(1)} %reshape.78.index_ref, f32[2048,256]{1,0:T(8,128)S(1)} %own.1.base_ref, bf16[1280,256]{1,0:T(8,128)(2,1)S(1)} %bitcast.13), custom_call_target="tpu_custom_call" | custom-call | tf_op jit(solution)/shard_map/finish/pallas_call | solution.py:416
  88.9 4.5 %all-to-all-done.2 = bf16[16,16,256]{2,1,0:T(8,128)(2,1)S(1)} async-done(((bf16[16,16,256]{2,1,0:T(8,128)(2,1)}), bf16[16,16,256]{2,1,0:T(8,128)(2,1)S(1)}, u32[]{:S(2)}, u32[]{:S(2)}) %all-to-all-start.2) | async-done | bytes 131104 | tf_op jit(solution)/shard_map/all_to_all | solution.py:349
  93.4 0.0 collective-permute-start.2
  93.4 1.3 %collective-permute-done.2 = bf16[256,256]{1,0:T(8,128)(2,1)S(1)} collective-permute-done((bf16[256,256]{1,0:T(8,128)(2,1)S(1)}, bf16[256,256]{1,0:T(8,128)(2,1)S(1)}, u32[]{:S(2)}, u32[]{:S(2)}) %collective-permute-start.2) | collective-permute-done | bytes 131104 | tf_op jit(solution)/shard_map/ppermute | solution.py:430
  94.8 0.8 select_convert_fusion
  (9 shorter events, 0.1 us)
Async XLA Ops:
  0.6 0.7 copy-start.3
  1.3 0.7 copy-start.5
  2.0 12.2 %copy-start.7 = (s32[65536]{0:T(1024)S(1)}, s32[65536]{0:T(1024)}, u32[]{:S(2)}) copy-start(s32[65536]{0:T(1024)} %param.15) | copy-start | bytes 786436
  2.0 12.2 %copy-start.8 = (s32[65536]{0:T(1024)S(1)}, s32[65536]{0:T(1024)}, u32[]{:S(2)}) copy-start(s32[65536]{0:T(1024)} %param.14) | copy-start | bytes 786436
  6.8 29.3 %all-to-all-start = ((bf16[32,48,256]{2,1,0:T(8,128)(2,1)}), bf16[32,48,256]{2,1,0:T(8,128)(2,1)S(1)}, u32[]{:S(2)}, u32[]{:S(2)}) async-start(bf16[32,48,256]{2,1,0:T(8,128)(2,1)} %bitcast.2), calls=%async_computation | async-start | bytes 1572864 | tf_op jit(solution)/shard_map/all_to_all | solution.py:239
  14.1 22.0 %copy-start = (bf16[2048,256]{1,0:T(8,128)(2,1)S(1)}, bf16[2048,256]{1,0:T(8,128)(2,1)}, u32[]{:S(2)}) copy-start(bf16[2048,256]{1,0:T(8,128)(2,1)} %feats_ref.3) | copy-start | bytes 3145732
  14.1 22.0 %copy-start.1 = (bf16[256,256]{1,0:T(8,128)(2,1)S(1)}, bf16[256,256]{1,0:T(8,128)(2,1)}, u32[]{:S(2)}) copy-start(bf16[256,256]{1,0:T(8,128)(2,1)} %ws_ref.3) | copy-start | bytes 393220
  14.1 22.0 %copy-start.2 = (bf16[256,256]{1,0:T(8,128)(2,1)S(1)}, bf16[256,256]{1,0:T(8,128)(2,1)}, u32[]{:S(2)}) copy-start(bf16[256,256]{1,0:T(8,128)(2,1)} %wn_ref.1) | copy-start | bytes 393220
  48.3 8.2 %collective-permute-start = (f32[256,256]{1,0:T(8,128)S(1)}, f32[256,256]{1,0:T(8,128)S(1)}, u32[]{:S(2)}, u32[]{:S(2)}) collective-permute-start(f32[256,256]{1,0:T(8,128)S(1)} %constant_dynamic-slice_fusion), channel_id=1, source_target_pairs={{0,8},{8,0},{16,24},{24,16},{1,9},{9,1},{17,25},{25,17},{2,10},{10... | collective-permute-start | bytes 786440 | tf_op jit(solution)/shard_map/ppermute | solution.py:369
  52.2 4.4 %collective-permute-start.1 = (bf16[768,256]{1,0:T(8,128)(2,1)S(1)}, bf16[768,256]{1,0:T(8,128)(2,1)S(1)}, u32[]{:S(2)}, u32[]{:S(2)}) collective-permute-start(bf16[768,256]{1,0:T(8,128)(2,1)S(1)} %far.2), channel_id=1, source_target_pairs={{0,8},{8,0},{16,24},{24,16},{1,9},{9,1},{17,25},{25,17},{2,10},{10... | collective-permute-start | bytes 1179656 | tf_op jit(solution)/shard_map/ppermute | solution.py:371
  56.7 6.7 %copy-start.4 = (s32[512]{0:T(512)S(1)}, s32[512]{0:T(512)}, u32[]{:S(2)}) copy-start(s32[512]{0:T(512)} %send_ref.1) | copy-start | bytes 6148
  57.6 23.8 %all-to-all-start.1 = ((bf16[16,80,256]{2,1,0:T(8,128)(2,1)}), bf16[16,80,256]{2,1,0:T(8,128)(2,1)S(1)}, u32[]{:S(2)}, u32[]{:S(2)}) async-start(bf16[16,80,256]{2,1,0:T(8,128)(2,1)} %pad_maximum_fusion), calls=%async_computation.1 | async-start | bytes 1310720 | tf_op jit(solution)/shard_map/all_to_all | solution.py:349
  63.5 22.2 %copy-start.6 = (s32[32]{0:T(128)S(1)}, s32[32]{0:T(128)}, u32[]{:S(2)}) copy-start(s32[32]{0:T(128)} %hub_ref.1) | copy-start | bytes 388
  82.1 11.3 %all-to-all-start.2 = ((bf16[16,16,256]{2,1,0:T(8,128)(2,1)}), bf16[16,16,256]{2,1,0:T(8,128)(2,1)S(1)}, u32[]{:S(2)}, u32[]{:S(2)}) async-start(bf16[16,16,256]{2,1,0:T(8,128)(2,1)} %broadcast_in_dim.6), calls=%async_computation.2 | async-start | bytes 262144 | tf_op jit(solution)/shard_map/all_to_all | solution.py:349
  93.4 1.3 %collective-permute-start.2 = (bf16[256,256]{1,0:T(8,128)(2,1)S(1)}, bf16[256,256]{1,0:T(8,128)(2,1)S(1)}, u32[]{:S(2)}, u32[]{:S(2)}) collective-permute-start(bf16[256,256]{1,0:T(8,128)(2,1)S(1)} %bitcast.20), channel_id=1, source_target_pairs={{0,8},{8,0},{16,24},{24,16},{1,9},{9,1},{17,25},{25,17},{2,10},{10... | collective-permute-start | bytes 393224 | tf_op jit(solution)/shard_map/ppermute | solution.py:430

commit v4 on v3

--- a/solution.py
+++ b/solution.py
@@ -11,6 +11,7 @@
 AXES = ("dom", "sub")
 T = 256
 LANES = 128
+PACKED = 16
 F8 = jnp.float8_e4m3fn
 
 
@@ -26,8 +27,8 @@
     return jnp.dot(a, b, preferred_element_type=jnp.float32)
 
 
-def counts_kernel(first_ref, last_ref, flag_ref, keys_ref, adj_ref, deg_ref, tile_ref,
-                  *, all_tiles, window, unroll):
+def counts_kernel(first_ref, last_ref, flag_ref, keys_ref, near_ref, far_ref, deg_ref, tile_ref,
+                  *, own_tiles, all_tiles, window):
     block = pl.program_id(0)
     key_rows = keys_ref.shape[0]
     ids = (lax.broadcasted_iota(jnp.int32, (T, LANES), 0) - 128).astype(jnp.int8)
@@ -51,42 +52,50 @@
 
     deg_ref[...] = jnp.zeros_like(deg_ref)
 
-    def build(j, carry):
-        tile = block * all_tiles + j
-        start = jnp.minimum(first_ref[tile], key_rows - window)
-        counts = tile_part(tile, start, window)
-        deg_ref[...] += counts[:, :LANES] + counts[:, LANES:]
-        adj_ref[:, pl.ds(pl.multiple_of(j * T, T), T)] = counts.astype(jnp.bfloat16)
-        return carry
-
-    lax.fori_loop(0, all_tiles, build, 0, unroll=unroll)
+    ranges = [(near_ref, 0, own_tiles), (far_ref, own_tiles, all_tiles - own_tiles)]
+
+    for ref, shift, number in ranges:
+
+        def build(j, carry, ref=ref, shift=shift):
+            tile = block * all_tiles + shift + j
+            start = jnp.minimum(first_ref[tile], key_rows - window)
+            counts = tile_part(tile, start, window)
+            deg_ref[...] += counts[:, :LANES] + counts[:, LANES:]
+            ref[:, pl.ds(pl.multiple_of(j * T, T), T)] = counts.astype(jnp.bfloat16)
+            return carry
+
+        unroll = max(u for u in range(1, 13) if number % u == 0)
+        lax.fori_loop(0, number, build, 0, unroll=unroll)
 
     @pl.when(flag_ref[block] > 0)
     def _():
-        def rest(j, carry):
-            tile = block * all_tiles + j
-            start = jnp.minimum(first_ref[tile], key_rows - window)
-            stop = last_ref[tile]
-
-            @pl.when(stop > start + window)
-            def _():
-                tile_ref[...] = tile_part(tile, start, window)
-
-                def more(row, inner):
-                    counts = tile_part(tile, row, 1)
-                    deg_ref[...] += counts[:, :LANES] + counts[:, LANES:]
-                    tile_ref[...] += counts
-                    return inner
-
-                lax.fori_loop(start + window, stop, more, 0)
-                adj_ref[:, pl.ds(pl.multiple_of(j * T, T), T)] = tile_ref[...].astype(jnp.bfloat16)
-
-            return carry
-
-        lax.fori_loop(0, all_tiles, rest, 0)
-
-
-def forward_kernel(core_ref, adj_ref, deg_ref, feats_ref, remote_ref, ws_ref, wn_ref, cot_ref,
+        for ref, shift, number in ranges:
+
+            def rest(j, carry, ref=ref, shift=shift):
+                tile = block * all_tiles + shift + j
+                start = jnp.minimum(first_ref[tile], key_rows - window)
+                stop = last_ref[tile]
+
+                @pl.when(stop > start + window)
+                def _():
+                    tile_ref[...] = tile_part(tile, start, window)
+
+                    def more(row, inner):
+                        counts = tile_part(tile, row, 1)
+                        deg_ref[...] += counts[:, :LANES] + counts[:, LANES:]
+                        tile_ref[...] += counts
+                        return inner
+
+                    lax.fori_loop(start + window, stop, more, 0)
+                    cols = pl.ds(pl.multiple_of(j * T, T), T)
+                    ref[:, cols] = tile_ref[...].astype(jnp.bfloat16)
+
+                return carry
+
+            lax.fori_loop(0, number, rest, 0)
+
+
+def forward_kernel(core_ref, near_ref, far_ref, deg_ref, feats_ref, remote_ref, ws_ref, wn_ref, cot_ref,
                    out_ref, g_ref, dmsg_ref, grads_ref, table_ref, *, chunk):
     block = pl.program_id(0)
     pairs = remote_ref.shape[0] // chunk // 2
@@ -101,8 +110,7 @@
                 ]
 
     rows, width = out_ref.shape
-    own = feats_ref.shape[0]
-    total = mm(adj_ref[:, :own], feats_ref[...]) + mm(adj_ref[:, own:], table_ref[...])
+    total = mm(near_ref[...], feats_ref[...]) + mm(far_ref[...], table_ref[...])
     degree = jnp.sum(deg_ref[...], axis=1, keepdims=True)
     inverse = 1.0 / jnp.maximum(degree, 1.0)
     mean = (total * inverse).astype(jnp.bfloat16)
@@ -147,30 +155,23 @@
     out_ref[...] = (base_ref[...] + mm(pick, back_ref[...])).astype(jnp.bfloat16)
 
 
-def gather_kernel(hub_ref, send_ref, feats_ref, out_ref, wide_ref, hubs_ref, sends_ref):
-    hub_dev = hubs_ref.shape[0]
-    count = sends_ref.shape[0]
-    devices = (out_ref.shape[0] - count) // hub_dev
-    cap = count // devices
+def gather_kernel(hub_ref, send_ref, feats_ref, out_ref, wide_ref, *, devices):
+    hub_dev = hub_ref.shape[0]
+    cap = send_ref.shape[0] // devices
     pack = hub_dev + cap
     wide_ref[...] = feats_ref[...].astype(jnp.float32)
 
-    def hub(i, carry):
-        hubs_ref[pl.ds(i, 1), :] = wide_ref[pl.ds(hub_ref[i], 1), :]
-        return carry
-
-    def send(i, carry):
-        sends_ref[pl.ds(i, 1), :] = wide_ref[pl.ds(send_ref[i], 1), :]
-        return carry
-
-    lax.fori_loop(0, hub_dev, hub, 0, unroll=8)
-    lax.fori_loop(0, count, send, 0, unroll=16)
-    hubs = hubs_ref[...].astype(jnp.bfloat16)
+    def rows(index_ref, start):
+        picked = [wide_ref[pl.ds(index_ref[start + i], 1), :] for i in range(PACKED)]
+        return jnp.concatenate(picked, axis=0).astype(jnp.bfloat16)
+
+    hubs = jnp.concatenate([rows(hub_ref, i) for i in range(0, hub_dev, PACKED)], axis=0)
 
     def place(p, carry):
-        out_ref[pl.ds(pl.multiple_of(p * pack, 16), hub_dev), :] = hubs
-        halo = sends_ref[pl.ds(pl.multiple_of(p * cap, 16), cap), :].astype(jnp.bfloat16)
-        out_ref[pl.ds(pl.multiple_of(p * pack + hub_dev, 16), cap), :] = halo
+        at = pl.multiple_of(p * pack, PACKED)
+        out_ref[pl.ds(at, hub_dev), :] = hubs
+        for i in range(0, cap, PACKED):
+            out_ref[pl.ds(at + hub_dev + i, PACKED), :] = rows(send_ref, p * cap + i)
         return carry
 
     lax.fori_loop(0, devices, place, 0, unroll=4)
@@ -213,7 +214,7 @@
 
     send_table = send_rows.reshape(devices, cap)
     outgoing = pl.pallas_call(
-        gather_kernel,
+        functools.partial(gather_kernel, devices=devices),
         name="gather",
         out_shape=jax.ShapeDtypeStruct((far, width), bf16),
         grid_spec=pltpu.PrefetchScalarGridSpec(
@@ -221,19 +222,15 @@
             grid=(1,),
             in_specs=[pl.BlockSpec((vcount, width), lambda b, *_: (0, 0))],
             out_specs=pl.BlockSpec((far, width), lambda b, *_: (0, 0)),
-            scratch_shapes=[
-                pltpu.VMEM((vcount, width), f32),
-                pltpu.VMEM((hub_dev, width), f32),
-                pltpu.VMEM((devices * cap, width), f32),
-            ],
+            scratch_shapes=[pltpu.VMEM((vcount, width), f32)],
         ),
         compiler_params=pltpu.CompilerParams(
             dimension_semantics=("arbitrary",),
             vmem_limit_bytes=(4 << 20) + width * (8 * vcount + 8 * far),
         ),
     )(
-        hub_rows,
-        send_rows,
+        pltpu.with_memory_space_constraint(hub_rows, pltpu.HBM),
+        pltpu.with_memory_space_constraint(send_rows, pltpu.HBM),
         pltpu.with_memory_space_constraint(feats, pltpu.HBM),
     ).reshape(devices, pack, width)
     remote = lax.all_to_all(outgoing, AXES, split_axis=0, concat_axis=0, tiled=True)
@@ -264,13 +261,15 @@
     window = min(key_rows, math.ceil((average + LANES + 2.0 * math.sqrt(average)) / LANES))
     over = (last > jnp.minimum(first, key_rows - window) + window).astype(jnp.int32)
     flags = jnp.max(over.reshape(own_tiles, all_tiles), axis=1)
-    unroll = max(u for u in range(1, 17) if all_tiles % u == 0)
-
-    adj, deg = pl.pallas_call(
-        functools.partial(counts_kernel, all_tiles=all_tiles, window=window, unroll=unroll),
+
+    near, away, deg = pl.pallas_call(
+        functools.partial(
+            counts_kernel, own_tiles=own_tiles, all_tiles=all_tiles, window=window
+        ),
         name="counts",
         out_shape=(
-            pltpu.HBM((vcount, slots), bf16),
+            pltpu.HBM((vcount, vcount), bf16),
+            pltpu.HBM((vcount, far), bf16),
             pltpu.HBM((vcount, LANES), f32),
         ),
         grid_spec=pltpu.PrefetchScalarGridSpec(
@@ -278,7 +277,8 @@
             grid=(own_tiles,),
             in_specs=[pl.BlockSpec((key_rows, LANES), lambda b, *_: (0, 0))],
             out_specs=[
-                pl.BlockSpec((T, slots), lambda b, *_: (b, 0)),
+                pl.BlockSpec((T, vcount), lambda b, *_: (b, 0)),
+                pl.BlockSpec((T, far), lambda b, *_: (b, 0)),
                 pl.BlockSpec((T, LANES), lambda b, *_: (b, 0)),
             ],
             scratch_shapes=[pltpu.VMEM((T, T), f32)],
@@ -288,7 +288,8 @@
         ),
     )(first, last, flags, keys)
 
-    adj = pltpu.with_memory_space_constraint(adj, pltpu.HBM)
+    near = pltpu.with_memory_space_constraint(near, pltpu.HBM)
+    away = pltpu.with_memory_space_constraint(away, pltpu.HBM)
     deg = pltpu.with_memory_space_constraint(deg, pltpu.HBM)
     whole = lambda b, *_: (0, 0)
     by_row = lambda b, *_: (b, 0)
@@ -300,7 +301,8 @@
             num_scalar_prefetch=1,
             grid=(vcount // rows,),
             in_specs=[
-                pl.BlockSpec((rows, slots), by_row),
+                pl.BlockSpec((rows, vcount), by_row),
+                pl.BlockSpec((rows, far), by_row),
                 pl.BlockSpec((rows, LANES), by_row),
                 pl.BlockSpec((vcount, width), whole),
                 pl.BlockSpec((far, width), whole),
@@ -328,7 +330,8 @@
         ),
     )(
         jnp.reshape(core, (1,)).astype(jnp.int32),
-        adj,
+        near,
+        away,
         deg,
         feats,
         remote,
@@ -350,27 +353,30 @@
             x, AXES, split_axis=0, concat_axis=0, axis_index_groups=groups, tiled=True
         )
 
-    def far_part(start, dmsg):
+    far_cols = max(c for c in range(T, 4 * T, T) if far // 2 % c == 0)
+    far_steps = far // 2 // far_cols
+
+    def far_part(side, dmsg):
         return call(
             far_kernel,
-            (far // 2 // T,),
+            (far_steps,),
             [
-                pl.BlockSpec((vcount, T), lambda j: (0, j + start // T)),
+                pl.BlockSpec((vcount, far_cols), lambda j: (0, j + side * far_steps)),
                 pl.BlockSpec((vcount, width), whole),
             ],
-            pl.BlockSpec((T, width), by_row),
+            pl.BlockSpec((far_cols, width), by_row),
             jax.ShapeDtypeStruct((far // 2, width), bf16),
             "far",
-            16 << 20,
-        )(adj, dmsg)
+            24 << 20,
+        )(away, dmsg)
 
     sent = lax.dynamic_slice_in_dim(parts, (1 - core) * width, width, 0)
     kept = lax.dynamic_slice_in_dim(parts, core * width, width, 0)
     came = lax.ppermute(sent, "dom", twin)
-    given = far_part(vcount + far // 2, dmsg)
+    given = far_part(1, dmsg)
     got = lax.ppermute(given, "dom", twin)
     dmsg, given = tie(dmsg, given)
-    kept_slots = far_part(vcount, dmsg)
+    kept_slots = far_part(0, dmsg)
     came, kept_slots = tie(came, kept_slots)
     share = width // half
     piece = (kept + came).astype(bf16).reshape(half, share, width)
@@ -396,19 +402,19 @@
         jax.ShapeDtypeStruct((vcount, width), f32),
         "own",
         16 << 20,
-    )(adj, dmsg, g, w_self)
+    )(near, dmsg, g, w_self)
 
     mine = jnp.sum(returned[:, bundle - share :].astype(f32), axis=0).astype(bf16)
     mine, base = tie(mine, base)
     mine = exchange(jnp.broadcast_to(mine[None], (half, share, width))).reshape(width, width)
     table = send_rows.reshape(dom // 2, 2, sub, cap)
-    near = lax.dynamic_index_in_dim(table, core, 1, keepdims=False).reshape(half, cap)
-    away = lax.dynamic_index_in_dim(table, 1 - core, 1, keepdims=False).reshape(half, cap)
+    same = lax.dynamic_index_in_dim(table, core, 1, keepdims=False).reshape(half, cap)
+    cross = lax.dynamic_index_in_dim(table, 1 - core, 1, keepdims=False).reshape(half, cap)
     index = jnp.concatenate(
         [
             jnp.broadcast_to(hub_rows[None], (half, hub_dev)),
-            near,
-            away,
+            same,
+            cross,
             jnp.full((half, share), -1, jnp.int32),
         ],
         axis=1,

time: 96.2 us -> 93.5 us (0.972)
  Pallas kernels: 45.2 us -> 43.3 us
  local copies, waits for them, and re-layouts: 2.55 us -> 1.22 us
    pallas_call x4, Pallas kernels: 23.1 us -> 21.2 us  [the longest x1 10.6 us: body(): pl.pallas_call(functools.partial(counts_kernel, own_tiles=own_tiles, all_...]
    unnamed x18 -> x14, local copies, waits for them, and re-layouts: 1.37 us -> 0.04 us
where the time goes in v4:
time: 93.5 us; the launch traced here: 92.5 us
  Pallas kernels  43.3 us (46%)
  waiting for transfers between devices  18.1 us (19%)
  starting transfers between devices  17.1 us (18%)
  other arithmetic  11.8 us (13%)
  local copies, waits for them, and re-layouts  1.22 us (1%)
    all_to_all x2, waiting for transfers between devices, exchange(): lax.all_to_all(x, AXES, split_axis=0, concat_axis=0, axis_index_groups=gr...  15.6 us
    pallas_call x1, Pallas kernels, body(): pl.pallas_call(functools.partial(forward_kernel, chunk=sub * pack), name=...  12.3 us
    pallas_call x1, Pallas kernels, body(): pl.pallas_call(functools.partial(counts_kernel, own_tiles=own_tiles, all_...  10.6 us
    all_to_all x2, starting transfers between devices, exchange(): lax.all_to_all(x, AXES, split_axis=0, concat_axis=0, axis_index_groups=gr...  9.21 us
    sort x1, other arithmetic, body(): keys = lax.sort(key, is_stable=False).reshape(key_rows, LANES)  8.79 us
    all_to_all x1, starting transfers between devices, body(): lax.all_to_all(outgoing, AXES, split_axis=0, concat_axis=0, tiled=True)  7.3 us
    pallas_call x1, Pallas kernels, body(): call(own_kernel, (vcount // cols,), [pl.BlockSpec((vcount, cols), lambda...  6.89 us
    pallas_call x2, Pallas kernels, far_part(): call(far_kernel, (far_steps,), [pl.BlockSpec((vcount, far_cols), lambda j...  6.39 us
  transfers between devices with their start and end apart: 6, of which 4 were waited for; matrix products, arithmetic and copies ran while one was open for 11% of the time, Pallas kernels for 29%

profile of v4, /device:TPU:0, one launch (start us, length us, event | category | flops | bytes accessed | tf_op | source)
XLA Modules:
  0.0 92.5 jit_solution(9659300936767507730)
XLA Ops:
  0.6 0.0 copy-start.3
  0.6 0.0 copy-start.4
  0.7 4.2 %gather.1 = bf16[1536,256]{1,0:T(8,128)(2,1)} custom-call(s32[32]{0:T(128)} %hub_ref.1, s32[512]{0:T(512)} %send_ref.1, bf16[2048,256]{1,0:T(8,128)(2,1)} %feats_ref.3), custom_call_target="tpu_custom_call" | custom-call | tf_op jit(solution)/shard_map/gather/pallas_call | solution.py:216
  4.9 7.3 %all-to-all-start = ((bf16[32,48,256]{2,1,0:T(8,128)(2,1)}), bf16[32,48,256]{2,1,0:T(8,128)(2,1)S(1)}, u32[]{:S(2)}, u32[]{:S(2)}) async-start(bf16[32,48,256]{2,1,0:T(8,128)(2,1)} %bitcast.2), calls=%async_computation | async-start | bytes 1572864 | tf_op jit(solution)/shard_map/all_to_all | solution.py:236
  12.2 0.0 copy-start
  12.2 0.0 copy-start.1
  12.2 0.0 copy-start.2
  12.2 0.0 copy-done.3
  12.2 0.0 copy-done.4
  12.2 0.6 and_or_fusion
  12.9 8.8 %sort.7 = s32[65536]{0:T(1024)S(1)} sort(s32[65536]{0:T(1024)S(1)} %and_or_fusion), dimensions={0}, to_apply=%region_0.1 | sort | flops 1048576 | bytes 524288 | tf_op jit(solution)/shard_map/sort | solution.py:254
  21.7 0.1 slice_reduce_fusion
  21.8 0.2 convert_reduce_fusion
  22.0 0.1 compare_convert_fusion
  22.1 0.1 reshape.80
  22.2 0.1 reduce_max.9.flag_ref
  22.3 0.1 fusion.14
  22.4 10.6 %counts.1 = (bf16[2048,2048]{1,0:T(8,128)(2,1)}, bf16[2048,1536]{1,0:T(8,128)(2,1)}, f32[2048,128]{1,0:T(8,128)}) custom-call(s32[112]{0:T(128)S(1)} %get-tuple-element.37.first_ref, s32[112]{0:T(128)S(1)} %get-tuple-element.36.last_ref, s32[8]{0:T(128)S(1)} %reduce_max.9.flag_ref, s32[512,128]{1,0:T(8,128)S(1)} %bitcast.16), custom_call_target="tpu_custom_call" | custom-call | tf_op jit(solution)/shard_map/counts/pallas_call | solution.py:265
  33.0 1.2 %all-to-all-done = bf16[32,48,256]{2,1,0:T(8,128)(2,1)S(1)} async-done(((bf16[32,48,256]{2,1,0:T(8,128)(2,1)}), bf16[32,48,256]{2,1,0:T(8,128)(2,1)S(1)}, u32[]{:S(2)}, u32[]{:S(2)}) %all-to-all-start) | async-done | bytes 786464 | tf_op jit(solution)/shard_map/all_to_all | solution.py:236
  34.2 0.0 copy-done
  34.2 0.0 copy-done.1
  34.2 0.0 copy-done.2
  34.2 12.3 %forward.1 = (bf16[2048,256]{1,0:T(8,128)(2,1)}, bf16[2048,256]{1,0:T(8,128)(2,1)}, bf16[2048,256]{1,0:T(8,128)(2,1)}, f32[512,256]{1,0:T(8,128)S(1)}) custom-call(s32[1]{0:T(128)} %bitcast.core_ref, bf16[2048,2048]{1,0:T(8,128)(2,1)} %get-tuple-element.18.near_ref.adj_ref, bf16[2048,1536]{1,0:T(8,128)(2,1)} %get-tuple-element.19.far_ref.adj_ref, ...), custom_call_target="tpu_custom_call" | custom-call | tf_op jit(solution)/shard_map/forward/pallas_call | solution.py:297
  46.4 0.1 collective-permute-start
  46.5 3.2 %far.2 = bf16[768,256]{1,0:T(8,128)(2,1)S(1)} custom-call(bf16[2048,1536]{1,0:T(8,128)(2,1)} %get-tuple-element.19.far_ref.adj_ref, bf16[2048,256]{1,0:T(8,128)(2,1)} %get-tuple-element.24.dmsg_ref), custom_call_target="tpu_custom_call" | custom-call | tf_op jit(solution)/shard_map/far/pallas_call | solution.py:360
  49.7 0.6 collective-permute-start.1
  50.3 3.2 %far.3 = bf16[768,256]{1,0:T(8,128)(2,1)S(1)} custom-call(bf16[2048,1536]{1,0:T(8,128)(2,1)} %get-tuple-element.19.far_ref.adj_ref, bf16[2048,256]{1,0:T(8,128)(2,1)} %get-tuple-element.24.dmsg_ref), custom_call_target="tpu_custom_call" | custom-call | tf_op jit(solution)/shard_map/far/pallas_call | solution.py:360
  53.5 0.0 collective-permute-done
  53.6 0.0 collective-permute-done.1
  53.6 0.1 add_convert_fusion
  53.7 0.0 copy-start.5
  53.7 0.9 pad_maximum_fusion
  54.6 5.7 %all-to-all-start.1 = ((bf16[16,80,256]{2,1,0:T(8,128)(2,1)}), bf16[16,80,256]{2,1,0:T(8,128)(2,1)S(1)}, u32[]{:S(2)}, u32[]{:S(2)}) async-start(bf16[16,80,256]{2,1,0:T(8,128)(2,1)} %pad_maximum_fusion), calls=%async_computation.1 | async-start | bytes 1310720 | tf_op jit(solution)/shard_map/all_to_all | solution.py:352
  60.3 0.0 copy-done.5
  60.3 0.1 reshape.75
  60.3 0.0 copy-start.6
  60.3 6.9 %own.1.base_ref = f32[2048,256]{1,0:T(8,128)S(1)} custom-call(bf16[2048,2048]{1,0:T(8,128)(2,1)} %get-tuple-element.18.near_ref.adj_ref, bf16[2048,256]{1,0:T(8,128)(2,1)} %get-tuple-element.24.dmsg_ref, bf16[2048,256]{1,0:T(8,128)(2,1)} %get-tuple-element.27.g_ref, bf16[256,256]{1,0:T(8,128)(2,1)S(1)} %copy-done.1), custom_call_target="tpu_custom_call" | custom-call | tf_op jit(solution)/shard_map/own/pallas_call | solution.py:392
  67.2 11.1 %all-to-all-done.1 = bf16[16,80,256]{2,1,0:T(8,128)(2,1)S(1)} async-done(((bf16[16,80,256]{2,1,0:T(8,128)(2,1)}), bf16[16,80,256]{2,1,0:T(8,128)(2,1)S(1)}, u32[]{:S(2)}, u32[]{:S(2)}) %all-to-all-start.1) | async-done | bytes 655392 | tf_op jit(solution)/shard_map/all_to_all | solution.py:352
  78.3 0.7 broadcast_in_dim.6
  79.0 3.5 %all-to-all-start.2 = ((bf16[16,16,256]{2,1,0:T(8,128)(2,1)}), bf16[16,16,256]{2,1,0:T(8,128)(2,1)S(1)}, u32[]{:S(2)}, u32[]{:S(2)}) async-start(bf16[16,16,256]{2,1,0:T(8,128)(2,1)} %broadcast_in_dim.6), calls=%async_computation.2 | async-start | bytes 262144 | tf_op jit(solution)/shard_map/all_to_all | solution.py:352
  82.5 0.0 copy-done.6
  82.6 0.1 pad.3.clone
  82.6 0.1 add_add_fusion
  82.7 0.1 reshape.78.index_ref
  82.8 3.0 %finish.1 = bf16[2048,256]{1,0:T(8,128)(2,1)} custom-call(s32[1,1280]{1,0:T(1,128)S(1)} %reshape.78.index_ref, f32[2048,256]{1,0:T(8,128)S(1)} %own.1.base_ref, bf16[1280,256]{1,0:T(8,128)(2,1)S(1)} %bitcast.13), custom_call_target="tpu_custom_call" | custom-call | tf_op jit(solution)/shard_map/finish/pallas_call | solution.py:422
  85.8 4.5 %all-to-all-done.2 = bf16[16,16,256]{2,1,0:T(8,128)(2,1)S(1)} async-done(((bf16[16,16,256]{2,1,0:T(8,128)(2,1)}), bf16[16,16,256]{2,1,0:T(8,128)(2,1)S(1)}, u32[]{:S(2)}, u32[]{:S(2)}) %all-to-all-start.2) | async-done | bytes 131104 | tf_op jit(solution)/shard_map/all_to_all | solution.py:352
  90.3 0.0 collective-permute-start.2
  90.3 1.3 %collective-permute-done.2 = bf16[256,256]{1,0:T(8,128)(2,1)S(1)} collective-permute-done((bf16[256,256]{1,0:T(8,128)(2,1)S(1)}, bf16[256,256]{1,0:T(8,128)(2,1)S(1)}, u32[]{:S(2)}, u32[]{:S(2)}) %collective-permute-start.2) | collective-permute-done | bytes 131104 | tf_op jit(solution)/shard_map/ppermute | solution.py:436
  91.6 0.8 select_convert_fusion
  (9 shorter events, 0.1 us)
Async XLA Ops:
  0.6 11.6 %copy-start.3 = (s32[65536]{0:T(1024)S(1)}, s32[65536]{0:T(1024)}, u32[]{:S(2)}) copy-start(s32[65536]{0:T(1024)} %param.15) | copy-start | bytes 786436
  0.6 11.6 %copy-start.4 = (s32[65536]{0:T(1024)S(1)}, s32[65536]{0:T(1024)}, u32[]{:S(2)}) copy-start(s32[65536]{0:T(1024)} %param.14) | copy-start | bytes 786436
  4.9 29.3 %all-to-all-start = ((bf16[32,48,256]{2,1,0:T(8,128)(2,1)}), bf16[32,48,256]{2,1,0:T(8,128)(2,1)S(1)}, u32[]{:S(2)}, u32[]{:S(2)}) async-start(bf16[32,48,256]{2,1,0:T(8,128)(2,1)} %bitcast.2), calls=%async_computation | async-start | bytes 1572864 | tf_op jit(solution)/shard_map/all_to_all | solution.py:236
  12.2 22.0 %copy-start = (bf16[2048,256]{1,0:T(8,128)(2,1)S(1)}, bf16[2048,256]{1,0:T(8,128)(2,1)}, u32[]{:S(2)}) copy-start(bf16[2048,256]{1,0:T(8,128)(2,1)} %feats_ref.3) | copy-start | bytes 3145732
  12.2 22.0 %copy-start.1 = (bf16[256,256]{1,0:T(8,128)(2,1)S(1)}, bf16[256,256]{1,0:T(8,128)(2,1)}, u32[]{:S(2)}) copy-start(bf16[256,256]{1,0:T(8,128)(2,1)} %ws_ref.3) | copy-start | bytes 393220
  12.2 22.0 %copy-start.2 = (bf16[256,256]{1,0:T(8,128)(2,1)S(1)}, bf16[256,256]{1,0:T(8,128)(2,1)}, u32[]{:S(2)}) copy-start(bf16[256,256]{1,0:T(8,128)(2,1)} %wn_ref.1) | copy-start | bytes 393220
  46.4 7.0 %collective-permute-start = (f32[256,256]{1,0:T(8,128)S(1)}, f32[256,256]{1,0:T(8,128)S(1)}, u32[]{:S(2)}, u32[]{:S(2)}) collective-permute-start(f32[256,256]{1,0:T(8,128)S(1)} %constant_dynamic-slice_fusion), channel_id=1, source_target_pairs={{0,8},{8,0},{16,24},{24,16},{1,9},{9,1},{17,25},{25,17},{2,10},{10... | collective-permute-start | bytes 786440 | tf_op jit(solution)/shard_map/ppermute | solution.py:375
  49.7 3.8 %collective-permute-start.1 = (bf16[768,256]{1,0:T(8,128)(2,1)S(1)}, bf16[768,256]{1,0:T(8,128)(2,1)S(1)}, u32[]{:S(2)}, u32[]{:S(2)}) collective-permute-start(bf16[768,256]{1,0:T(8,128)(2,1)S(1)} %far.2), channel_id=1, source_target_pairs={{0,8},{8,0},{16,24},{24,16},{1,9},{9,1},{17,25},{25,17},{2,10},{10... | collective-permute-start | bytes 1179656 | tf_op jit(solution)/shard_map/ppermute | solution.py:377
  53.7 6.6 %copy-start.5 = (s32[512]{0:T(512)S(1)}, s32[512]{0:T(512)}, u32[]{:S(2)}) copy-start(s32[512]{0:T(512)} %send_ref.1) | copy-start | bytes 6148
  54.6 23.8 %all-to-all-start.1 = ((bf16[16,80,256]{2,1,0:T(8,128)(2,1)}), bf16[16,80,256]{2,1,0:T(8,128)(2,1)S(1)}, u32[]{:S(2)}, u32[]{:S(2)}) async-start(bf16[16,80,256]{2,1,0:T(8,128)(2,1)} %pad_maximum_fusion), calls=%async_computation.1 | async-start | bytes 1310720 | tf_op jit(solution)/shard_map/all_to_all | solution.py:352
  60.3 22.2 %copy-start.6 = (s32[32]{0:T(128)S(1)}, s32[32]{0:T(128)}, u32[]{:S(2)}) copy-start(s32[32]{0:T(128)} %hub_ref.1) | copy-start | bytes 388
  79.0 11.3 %all-to-all-start.2 = ((bf16[16,16,256]{2,1,0:T(8,128)(2,1)}), bf16[16,16,256]{2,1,0:T(8,128)(2,1)S(1)}, u32[]{:S(2)}, u32[]{:S(2)}) async-start(bf16[16,16,256]{2,1,0:T(8,128)(2,1)} %broadcast_in_dim.6), calls=%async_computation.2 | async-start | bytes 262144 | tf_op jit(solution)/shard_map/all_to_all | solution.py:352
  90.3 1.3 %collective-permute-start.2 = (bf16[256,256]{1,0:T(8,128)(2,1)S(1)}, bf16[256,256]{1,0:T(8,128)(2,1)S(1)}, u32[]{:S(2)}, u32[]{:S(2)}) collective-permute-start(bf16[256,256]{1,0:T(8,128)(2,1)S(1)} %bitcast.20), channel_id=1, source_target_pairs={{0,8},{8,0},{16,24},{24,16},{1,9},{9,1},{17,25},{25,17},{2,10},{10... | collective-permute-start | bytes 393224 | tf_op jit(solution)/shard_map/ppermute | solution.py:436

commit v5 on v4

--- a/solution.py
+++ b/solution.py
@@ -102,6 +102,7 @@
 
     @pl.when(block == 0)
     def _():
+        grads_ref[...] = jnp.zeros_like(grads_ref)
         for half in range(2):
             for pair in range(pairs):
                 start = (2 * pair + (core_ref[0] ^ half)) * chunk
@@ -122,10 +123,6 @@
     g = (cot_ref[...].astype(jnp.float32) * slope).astype(jnp.bfloat16)
     g_ref[...] = g
     dmsg_ref[...] = (outer_nt(g, wn_ref[...]) * inverse).astype(jnp.bfloat16)
-
-    @pl.when(block == 0)
-    def _():
-        grads_ref[...] = jnp.zeros_like(grads_ref)
 
     grads_ref[:width, :] += outer_tn(mine, g)
     grads_ref[width:, :] += outer_tn(mean, g)

time: 93.5 us -> 92.4 us (0.988)
  no operation moved by 1% of the time
where the time goes in v5:
time: 92.4 us; the launch traced here: 91.9 us
  Pallas kernels  42.8 us (46%)
  waiting for transfers between devices  18.1 us (20%)
  starting transfers between devices  17.1 us (19%)
  other arithmetic  11.8 us (13%)
  local copies, waits for them, and re-layouts  1.22 us (1%)
    all_to_all x2, waiting for transfers between devices, exchange(): lax.all_to_all(x, AXES, split_axis=0, concat_axis=0, axis_index_groups=gr...  15.6 us
    pallas_call x1, Pallas kernels, body(): pl.pallas_call(functools.partial(forward_kernel, chunk=sub * pack), name=...  11.7 us
    pallas_call x1, Pallas kernels, body(): pl.pallas_call(functools.partial(counts_kernel, own_tiles=own_tiles, all_...  10.6 us
    all_to_all x2, starting transfers between devices, exchange(): lax.all_to_all(x, AXES, split_axis=0, concat_axis=0, axis_index_groups=gr...  9.2 us
    sort x1, other arithmetic, body(): keys = lax.sort(key, is_stable=False).reshape(key_rows, LANES)  8.79 us
    all_to_all x1, starting transfers between devices, body(): lax.all_to_all(outgoing, AXES, split_axis=0, concat_axis=0, tiled=True)  7.3 us
    pallas_call x1, Pallas kernels, body(): call(own_kernel, (vcount // cols,), [pl.BlockSpec((vcount, cols), lambda...  6.88 us
    pallas_call x2, Pallas kernels, far_part(): call(far_kernel, (far_steps,), [pl.BlockSpec((vcount, far_cols), lambda j...  6.39 us
  transfers between devices with their start and end apart: 6, of which 4 were waited for; matrix products, arithmetic and copies ran while one was open for 11% of the time, Pallas kernels for 29%

profile of v5, /device:TPU:0, one launch (start us, length us, event | category | flops | bytes accessed | tf_op | source)
XLA Modules:
  0.0 91.9 jit_solution(2213482483367315502)
XLA Ops:
  0.6 0.0 copy-start.3
  0.6 0.0 copy-start.4
  0.7 4.2 %gather.1 = bf16[1536,256]{1,0:T(8,128)(2,1)} custom-call(s32[32]{0:T(128)} %hub_ref.1, s32[512]{0:T(512)} %send_ref.1, bf16[2048,256]{1,0:T(8,128)(2,1)} %feats_ref.3), custom_call_target="tpu_custom_call" | custom-call | tf_op jit(solution)/shard_map/gather/pallas_call | solution.py:213
  4.9 7.3 %all-to-all-start = ((bf16[32,48,256]{2,1,0:T(8,128)(2,1)}), bf16[32,48,256]{2,1,0:T(8,128)(2,1)S(1)}, u32[]{:S(2)}, u32[]{:S(2)}) async-start(bf16[32,48,256]{2,1,0:T(8,128)(2,1)} %bitcast.2), calls=%async_computation | async-start | bytes 1572864 | tf_op jit(solution)/shard_map/all_to_all | solution.py:233
  12.2 0.0 copy-start
  12.2 0.0 copy-start.1
  12.2 0.0 copy-start.2
  12.2 0.0 copy-done.3
  12.2 0.0 copy-done.4
  12.2 0.6 and_or_fusion
  12.9 8.8 %sort.7 = s32[65536]{0:T(1024)S(1)} sort(s32[65536]{0:T(1024)S(1)} %and_or_fusion), dimensions={0}, to_apply=%region_0.1 | sort | flops 1048576 | bytes 524288 | tf_op jit(solution)/shard_map/sort | solution.py:251
  21.7 0.1 slice_reduce_fusion
  21.8 0.2 convert_reduce_fusion
  22.0 0.1 compare_convert_fusion
  22.1 0.1 reshape.80
  22.2 0.1 reduce_max.9.flag_ref
  22.3 0.1 fusion.14
  22.4 10.6 %counts.1 = (bf16[2048,2048]{1,0:T(8,128)(2,1)}, bf16[2048,1536]{1,0:T(8,128)(2,1)}, f32[2048,128]{1,0:T(8,128)}) custom-call(s32[112]{0:T(128)S(1)} %get-tuple-element.37.first_ref, s32[112]{0:T(128)S(1)} %get-tuple-element.36.last_ref, s32[8]{0:T(128)S(1)} %reduce_max.9.flag_ref, s32[512,128]{1,0:T(8,128)S(1)} %bitcast.16), custom_call_target="tpu_custom_call" | custom-call | tf_op jit(solution)/shard_map/counts/pallas_call | solution.py:262
  33.0 1.2 %all-to-all-done = bf16[32,48,256]{2,1,0:T(8,128)(2,1)S(1)} async-done(((bf16[32,48,256]{2,1,0:T(8,128)(2,1)}), bf16[32,48,256]{2,1,0:T(8,128)(2,1)S(1)}, u32[]{:S(2)}, u32[]{:S(2)}) %all-to-all-start) | async-done | bytes 786464 | tf_op jit(solution)/shard_map/all_to_all | solution.py:233
  34.2 0.0 copy-done
  34.2 0.0 copy-done.1
  34.2 0.0 copy-done.2
  34.2 11.7 %forward.1 = (bf16[2048,256]{1,0:T(8,128)(2,1)}, bf16[2048,256]{1,0:T(8,128)(2,1)}, bf16[2048,256]{1,0:T(8,128)(2,1)}, f32[512,256]{1,0:T(8,128)S(1)}) custom-call(s32[1]{0:T(128)} %bitcast.core_ref, bf16[2048,2048]{1,0:T(8,128)(2,1)} %get-tuple-element.18.near_ref.adj_ref, bf16[2048,1536]{1,0:T(8,128)(2,1)} %get-tuple-element.19.far_ref.adj_ref, ...), custom_call_target="tpu_custom_call" | custom-call | tf_op jit(solution)/shard_map/forward/pallas_call | solution.py:294
  45.9 0.1 collective-permute-start
  46.0 3.2 %far.2 = bf16[768,256]{1,0:T(8,128)(2,1)S(1)} custom-call(bf16[2048,1536]{1,0:T(8,128)(2,1)} %get-tuple-element.19.far_ref.adj_ref, bf16[2048,256]{1,0:T(8,128)(2,1)} %get-tuple-element.24.dmsg_ref), custom_call_target="tpu_custom_call" | custom-call | tf_op jit(solution)/shard_map/far/pallas_call | solution.py:357
  49.2 0.6 collective-permute-start.1
  49.7 3.2 %far.3 = bf16[768,256]{1,0:T(8,128)(2,1)S(1)} custom-call(bf16[2048,1536]{1,0:T(8,128)(2,1)} %get-tuple-element.19.far_ref.adj_ref, bf16[2048,256]{1,0:T(8,128)(2,1)} %get-tuple-element.24.dmsg_ref), custom_call_target="tpu_custom_call" | custom-call | tf_op jit(solution)/shard_map/far/pallas_call | solution.py:357
  52.9 0.0 collective-permute-done
  53.0 0.0 collective-permute-done.1
  53.0 0.1 add_convert_fusion
  53.1 0.0 copy-start.5
  53.1 0.9 pad_maximum_fusion
  54.0 5.7 %all-to-all-start.1 = ((bf16[16,80,256]{2,1,0:T(8,128)(2,1)}), bf16[16,80,256]{2,1,0:T(8,128)(2,1)S(1)}, u32[]{:S(2)}, u32[]{:S(2)}) async-start(bf16[16,80,256]{2,1,0:T(8,128)(2,1)} %pad_maximum_fusion), calls=%async_computation.1 | async-start | bytes 1310720 | tf_op jit(solution)/shard_map/all_to_all | solution.py:349
  59.7 0.0 copy-done.5
  59.7 0.1 reshape.75
  59.8 0.0 copy-start.6
  59.8 6.9 %own.1.base_ref = f32[2048,256]{1,0:T(8,128)S(1)} custom-call(bf16[2048,2048]{1,0:T(8,128)(2,1)} %get-tuple-element.18.near_ref.adj_ref, bf16[2048,256]{1,0:T(8,128)(2,1)} %get-tuple-element.24.dmsg_ref, bf16[2048,256]{1,0:T(8,128)(2,1)} %get-tuple-element.27.g_ref, bf16[256,256]{1,0:T(8,128)(2,1)S(1)} %copy-done.1), custom_call_target="tpu_custom_call" | custom-call | tf_op jit(solution)/shard_map/own/pallas_call | solution.py:389
  66.7 11.1 %all-to-all-done.1 = bf16[16,80,256]{2,1,0:T(8,128)(2,1)S(1)} async-done(((bf16[16,80,256]{2,1,0:T(8,128)(2,1)}), bf16[16,80,256]{2,1,0:T(8,128)(2,1)S(1)}, u32[]{:S(2)}, u32[]{:S(2)}) %all-to-all-start.1) | async-done | bytes 655392 | tf_op jit(solution)/shard_map/all_to_all | solution.py:349
  77.8 0.7 broadcast_in_dim.6
  78.4 3.5 %all-to-all-start.2 = ((bf16[16,16,256]{2,1,0:T(8,128)(2,1)}), bf16[16,16,256]{2,1,0:T(8,128)(2,1)S(1)}, u32[]{:S(2)}, u32[]{:S(2)}) async-start(bf16[16,16,256]{2,1,0:T(8,128)(2,1)} %broadcast_in_dim.6), calls=%async_computation.2 | async-start | bytes 262144 | tf_op jit(solution)/shard_map/all_to_all | solution.py:349
  82.0 0.0 copy-done.6
  82.0 0.1 pad.3.clone
  82.1 0.1 add_add_fusion
  82.2 0.1 reshape.78.index_ref
  82.2 3.0 %finish.1 = bf16[2048,256]{1,0:T(8,128)(2,1)} custom-call(s32[1,1280]{1,0:T(1,128)S(1)} %reshape.78.index_ref, f32[2048,256]{1,0:T(8,128)S(1)} %own.1.base_ref, bf16[1280,256]{1,0:T(8,128)(2,1)S(1)} %bitcast.13), custom_call_target="tpu_custom_call" | custom-call | tf_op jit(solution)/shard_map/finish/pallas_call | solution.py:419
  85.2 4.5 %all-to-all-done.2 = bf16[16,16,256]{2,1,0:T(8,128)(2,1)S(1)} async-done(((bf16[16,16,256]{2,1,0:T(8,128)(2,1)}), bf16[16,16,256]{2,1,0:T(8,128)(2,1)S(1)}, u32[]{:S(2)}, u32[]{:S(2)}) %all-to-all-start.2) | async-done | bytes 131104 | tf_op jit(solution)/shard_map/all_to_all | solution.py:349
  89.7 0.0 collective-permute-start.2
  89.7 1.3 %collective-permute-done.2 = bf16[256,256]{1,0:T(8,128)(2,1)S(1)} collective-permute-done((bf16[256,256]{1,0:T(8,128)(2,1)S(1)}, bf16[256,256]{1,0:T(8,128)(2,1)S(1)}, u32[]{:S(2)}, u32[]{:S(2)}) %collective-permute-start.2) | collective-permute-done | bytes 131104 | tf_op jit(solution)/shard_map/ppermute | solution.py:433
  91.1 0.8 select_convert_fusion
  (9 shorter events, 0.1 us)
Async XLA Ops:
  0.6 11.6 %copy-start.3 = (s32[65536]{0:T(1024)S(1)}, s32[65536]{0:T(1024)}, u32[]{:S(2)}) copy-start(s32[65536]{0:T(1024)} %param.15) | copy-start | bytes 786436
  0.6 11.6 %copy-start.4 = (s32[65536]{0:T(1024)S(1)}, s32[65536]{0:T(1024)}, u32[]{:S(2)}) copy-start(s32[65536]{0:T(1024)} %param.14) | copy-start | bytes 786436
  4.9 29.3 %all-to-all-start = ((bf16[32,48,256]{2,1,0:T(8,128)(2,1)}), bf16[32,48,256]{2,1,0:T(8,128)(2,1)S(1)}, u32[]{:S(2)}, u32[]{:S(2)}) async-start(bf16[32,48,256]{2,1,0:T(8,128)(2,1)} %bitcast.2), calls=%async_computation | async-start | bytes 1572864 | tf_op jit(solution)/shard_map/all_to_all | solution.py:233
  12.2 22.0 %copy-start = (bf16[2048,256]{1,0:T(8,128)(2,1)S(1)}, bf16[2048,256]{1,0:T(8,128)(2,1)}, u32[]{:S(2)}) copy-start(bf16[2048,256]{1,0:T(8,128)(2,1)} %feats_ref.3) | copy-start | bytes 3145732
  12.2 22.0 %copy-start.1 = (bf16[256,256]{1,0:T(8,128)(2,1)S(1)}, bf16[256,256]{1,0:T(8,128)(2,1)}, u32[]{:S(2)}) copy-start(bf16[256,256]{1,0:T(8,128)(2,1)} %ws_ref.3) | copy-start | bytes 393220
  12.2 22.0 %copy-start.2 = (bf16[256,256]{1,0:T(8,128)(2,1)S(1)}, bf16[256,256]{1,0:T(8,128)(2,1)}, u32[]{:S(2)}) copy-start(bf16[256,256]{1,0:T(8,128)(2,1)} %wn_ref.1) | copy-start | bytes 393220
  45.9 7.0 %collective-permute-start = (f32[256,256]{1,0:T(8,128)S(1)}, f32[256,256]{1,0:T(8,128)S(1)}, u32[]{:S(2)}, u32[]{:S(2)}) collective-permute-start(f32[256,256]{1,0:T(8,128)S(1)} %constant_dynamic-slice_fusion), channel_id=1, source_target_pairs={{0,8},{8,0},{16,24},{24,16},{1,9},{9,1},{17,25},{25,17},{2,10},{10... | collective-permute-start | bytes 786440 | tf_op jit(solution)/shard_map/ppermute | solution.py:372
  49.2 3.8 %collective-permute-start.1 = (bf16[768,256]{1,0:T(8,128)(2,1)S(1)}, bf16[768,256]{1,0:T(8,128)(2,1)S(1)}, u32[]{:S(2)}, u32[]{:S(2)}) collective-permute-start(bf16[768,256]{1,0:T(8,128)(2,1)S(1)} %far.2), channel_id=1, source_target_pairs={{0,8},{8,0},{16,24},{24,16},{1,9},{9,1},{17,25},{25,17},{2,10},{10... | collective-permute-start | bytes 1179656 | tf_op jit(solution)/shard_map/ppermute | solution.py:374
  53.1 6.6 %copy-start.5 = (s32[512]{0:T(512)S(1)}, s32[512]{0:T(512)}, u32[]{:S(2)}) copy-start(s32[512]{0:T(512)} %send_ref.1) | copy-start | bytes 6148
  54.0 23.8 %all-to-all-start.1 = ((bf16[16,80,256]{2,1,0:T(8,128)(2,1)}), bf16[16,80,256]{2,1,0:T(8,128)(2,1)S(1)}, u32[]{:S(2)}, u32[]{:S(2)}) async-start(bf16[16,80,256]{2,1,0:T(8,128)(2,1)} %pad_maximum_fusion), calls=%async_computation.1 | async-start | bytes 1310720 | tf_op jit(solution)/shard_map/all_to_all | solution.py:349
  59.8 22.2 %copy-start.6 = (s32[32]{0:T(128)S(1)}, s32[32]{0:T(128)}, u32[]{:S(2)}) copy-start(s32[32]{0:T(128)} %hub_ref.1) | copy-start | bytes 388
  78.4 11.3 %all-to-all-start.2 = ((bf16[16,16,256]{2,1,0:T(8,128)(2,1)}), bf16[16,16,256]{2,1,0:T(8,128)(2,1)S(1)}, u32[]{:S(2)}, u32[]{:S(2)}) async-start(bf16[16,16,256]{2,1,0:T(8,128)(2,1)} %broadcast_in_dim.6), calls=%async_computation.2 | async-start | bytes 262144 | tf_op jit(solution)/shard_map/all_to_all | solution.py:349
  89.7 1.3 %collective-permute-start.2 = (bf16[256,256]{1,0:T(8,128)(2,1)S(1)}, bf16[256,256]{1,0:T(8,128)(2,1)S(1)}, u32[]{:S(2)}, u32[]{:S(2)}) collective-permute-start(bf16[256,256]{1,0:T(8,128)(2,1)S(1)} %bitcast.20), channel_id=1, source_target_pairs={{0,8},{8,0},{16,24},{24,16},{1,9},{9,1},{17,25},{25,17},{2,10},{10... | collective-permute-start | bytes 393224 | tf_op jit(solution)/shard_map/ppermute | solution.py:433

commit v6 on v5

--- a/solution.py
+++ b/solution.py
@@ -110,13 +110,14 @@
                     pl.ds(pl.multiple_of(start, 16), chunk), :
                 ]
 
-    rows, width = out_ref.shape
+    rows = out_ref.shape[0]
     total = mm(near_ref[...], feats_ref[...]) + mm(far_ref[...], table_ref[...])
     degree = jnp.sum(deg_ref[...], axis=1, keepdims=True)
     inverse = 1.0 / jnp.maximum(degree, 1.0)
     mean = (total * inverse).astype(jnp.bfloat16)
     mine = feats_ref[pl.ds(pl.multiple_of(block * rows, rows), rows), :]
-    pre = mm(mine, ws_ref[...]) + mm(mean, wn_ref[...])
+    both = jnp.concatenate([mine, mean], axis=1)
+    pre = mm(both, jnp.concatenate([ws_ref[...], wn_ref[...]], axis=0))
     sig = jax.nn.sigmoid(pre)
     out_ref[...] = (pre * sig).astype(jnp.bfloat16)
     slope = sig * (1.0 + pre * (1.0 - sig))
@@ -124,8 +125,7 @@
     g_ref[...] = g
     dmsg_ref[...] = (outer_nt(g, wn_ref[...]) * inverse).astype(jnp.bfloat16)
 
-    grads_ref[:width, :] += outer_tn(mine, g)
-    grads_ref[width:, :] += outer_tn(mean, g)
+    grads_ref[...] += outer_tn(both, g)
 
 
 def far_kernel(adj_ref, dmsg_ref, *refs):

time: 92.4 us -> 92.2 us (level)
  no operation moved by 1% of the time
where the time goes in v6:
time: 92.2 us; the launch traced here: 91.5 us
  Pallas kernels  42.3 us (46%)
  waiting for transfers between devices  18.1 us (20%)
  starting transfers between devices  17.1 us (19%)
  other arithmetic  11.8 us (13%)
  local copies, waits for them, and re-layouts  1.22 us (1%)
    all_to_all x2, waiting for transfers between devices, exchange(): lax.all_to_all(x, AXES, split_axis=0, concat_axis=0, axis_index_groups=gr...  15.6 us
    pallas_call x1, Pallas kernels, body(): pl.pallas_call(functools.partial(forward_kernel, chunk=sub * pack), name=...  11.2 us
    pallas_call x1, Pallas kernels, body(): pl.pallas_call(functools.partial(counts_kernel, own_tiles=own_tiles, all_...  10.6 us
    all_to_all x2, starting transfers between devices, exchange(): lax.all_to_all(x, AXES, split_axis=0, concat_axis=0, axis_index_groups=gr...  9.21 us
    sort x1, other arithmetic, body(): keys = lax.sort(key, is_stable=False).reshape(key_rows, LANES)  8.79 us
    all_to_all x1, starting transfers between devices, body(): lax.all_to_all(outgoing, AXES, split_axis=0, concat_axis=0, tiled=True)  7.3 us
    pallas_call x1, Pallas kernels, body(): call(own_kernel, (vcount // cols,), [pl.BlockSpec((vcount, cols), lambda...  6.89 us
    pallas_call x2, Pallas kernels, far_part(): call(far_kernel, (far_steps,), [pl.BlockSpec((vcount, far_cols), lambda j...  6.39 us
  transfers between devices with their start and end apart: 6, of which 4 were waited for; matrix products, arithmetic and copies ran while one was open for 11% of the time, Pallas kernels for 29%

profile of v6, /device:TPU:0, one launch (start us, length us, event | category | flops | bytes accessed | tf_op | source)
XLA Modules:
  0.0 91.5 jit_solution(12374421645384175422)
XLA Ops:
  0.6 0.0 copy-start.3
  0.6 0.0 copy-start.4
  0.7 4.2 %gather.1 = bf16[1536,256]{1,0:T(8,128)(2,1)} custom-call(s32[32]{0:T(128)} %hub_ref.1, s32[512]{0:T(512)} %send_ref.1, bf16[2048,256]{1,0:T(8,128)(2,1)} %feats_ref.3), custom_call_target="tpu_custom_call" | custom-call | tf_op jit(solution)/shard_map/gather/pallas_call | solution.py:213
  4.9 7.3 %all-to-all-start = ((bf16[32,48,256]{2,1,0:T(8,128)(2,1)}), bf16[32,48,256]{2,1,0:T(8,128)(2,1)S(1)}, u32[]{:S(2)}, u32[]{:S(2)}) async-start(bf16[32,48,256]{2,1,0:T(8,128)(2,1)} %bitcast.2), calls=%async_computation | async-start | bytes 1572864 | tf_op jit(solution)/shard_map/all_to_all | solution.py:233
  12.2 0.0 copy-start
  12.2 0.0 copy-start.1
  12.2 0.0 copy-start.2
  12.2 0.0 copy-done.3
  12.2 0.0 copy-done.4
  12.2 0.6 and_or_fusion
  12.9 8.8 %sort.7 = s32[65536]{0:T(1024)S(1)} sort(s32[65536]{0:T(1024)S(1)} %and_or_fusion), dimensions={0}, to_apply=%region_0.1 | sort | flops 1048576 | bytes 524288 | tf_op jit(solution)/shard_map/sort | solution.py:251
  21.7 0.1 slice_reduce_fusion
  21.8 0.2 convert_reduce_fusion
  22.0 0.1 compare_convert_fusion
  22.1 0.1 reshape.80
  22.2 0.1 reduce_max.9.flag_ref
  22.3 0.1 fusion.14
  22.4 10.6 %counts.1 = (bf16[2048,2048]{1,0:T(8,128)(2,1)}, bf16[2048,1536]{1,0:T(8,128)(2,1)}, f32[2048,128]{1,0:T(8,128)}) custom-call(s32[112]{0:T(128)S(1)} %get-tuple-element.37.first_ref, s32[112]{0:T(128)S(1)} %get-tuple-element.36.last_ref, s32[8]{0:T(128)S(1)} %reduce_max.9.flag_ref, s32[512,128]{1,0:T(8,128)S(1)} %bitcast.16), custom_call_target="tpu_custom_call" | custom-call | tf_op jit(solution)/shard_map/counts/pallas_call | solution.py:262
  33.0 1.2 %all-to-all-done = bf16[32,48,256]{2,1,0:T(8,128)(2,1)S(1)} async-done(((bf16[32,48,256]{2,1,0:T(8,128)(2,1)}), bf16[32,48,256]{2,1,0:T(8,128)(2,1)S(1)}, u32[]{:S(2)}, u32[]{:S(2)}) %all-to-all-start) | async-done | bytes 786464 | tf_op jit(solution)/shard_map/all_to_all | solution.py:233
  34.2 0.0 copy-done
  34.2 0.0 copy-done.1
  34.2 0.0 copy-done.2
  34.2 11.2 %forward.1 = (bf16[2048,256]{1,0:T(8,128)(2,1)}, bf16[2048,256]{1,0:T(8,128)(2,1)}, bf16[2048,256]{1,0:T(8,128)(2,1)}, f32[512,256]{1,0:T(8,128)S(1)}) custom-call(s32[1]{0:T(128)} %bitcast.core_ref, bf16[2048,2048]{1,0:T(8,128)(2,1)} %get-tuple-element.18.near_ref.adj_ref, bf16[2048,1536]{1,0:T(8,128)(2,1)} %get-tuple-element.19.far_ref.adj_ref, ...), custom_call_target="tpu_custom_call" | custom-call | tf_op jit(solution)/shard_map/forward/pallas_call | solution.py:294
  45.4 0.1 collective-permute-start
  45.5 3.2 %far.2 = bf16[768,256]{1,0:T(8,128)(2,1)S(1)} custom-call(bf16[2048,1536]{1,0:T(8,128)(2,1)} %get-tuple-element.19.far_ref.adj_ref, bf16[2048,256]{1,0:T(8,128)(2,1)} %get-tuple-element.24.dmsg_ref), custom_call_target="tpu_custom_call" | custom-call | tf_op jit(solution)/shard_map/far/pallas_call | solution.py:357
  48.7 0.6 collective-permute-start.1
  49.3 3.2 %far.3 = bf16[768,256]{1,0:T(8,128)(2,1)S(1)} custom-call(bf16[2048,1536]{1,0:T(8,128)(2,1)} %get-tuple-element.19.far_ref.adj_ref, bf16[2048,256]{1,0:T(8,128)(2,1)} %get-tuple-element.24.dmsg_ref), custom_call_target="tpu_custom_call" | custom-call | tf_op jit(solution)/shard_map/far/pallas_call | solution.py:357
  52.5 0.0 collective-permute-done
  52.5 0.0 collective-permute-done.1
  52.6 0.1 add_convert_fusion
  52.6 0.0 copy-start.5
  52.7 0.9 pad_maximum_fusion
  53.5 5.7 %all-to-all-start.1 = ((bf16[16,80,256]{2,1,0:T(8,128)(2,1)}), bf16[16,80,256]{2,1,0:T(8,128)(2,1)S(1)}, u32[]{:S(2)}, u32[]{:S(2)}) async-start(bf16[16,80,256]{2,1,0:T(8,128)(2,1)} %pad_maximum_fusion), calls=%async_computation.1 | async-start | bytes 1310720 | tf_op jit(solution)/shard_map/all_to_all | solution.py:349
  59.2 0.0 copy-done.5
  59.3 0.1 reshape.75
  59.3 0.0 copy-start.6
  59.3 6.9 %own.1.base_ref = f32[2048,256]{1,0:T(8,128)S(1)} custom-call(bf16[2048,2048]{1,0:T(8,128)(2,1)} %get-tuple-element.18.near_ref.adj_ref, bf16[2048,256]{1,0:T(8,128)(2,1)} %get-tuple-element.24.dmsg_ref, bf16[2048,256]{1,0:T(8,128)(2,1)} %get-tuple-element.27.g_ref, bf16[256,256]{1,0:T(8,128)(2,1)S(1)} %copy-done.1), custom_call_target="tpu_custom_call" | custom-call | tf_op jit(solution)/shard_map/own/pallas_call | solution.py:389
  66.2 11.1 %all-to-all-done.1 = bf16[16,80,256]{2,1,0:T(8,128)(2,1)S(1)} async-done(((bf16[16,80,256]{2,1,0:T(8,128)(2,1)}), bf16[16,80,256]{2,1,0:T(8,128)(2,1)S(1)}, u32[]{:S(2)}, u32[]{:S(2)}) %all-to-all-start.1) | async-done | bytes 655392 | tf_op jit(solution)/shard_map/all_to_all | solution.py:349
  77.3 0.7 broadcast_in_dim.6
  78.0 3.5 %all-to-all-start.2 = ((bf16[16,16,256]{2,1,0:T(8,128)(2,1)}), bf16[16,16,256]{2,1,0:T(8,128)(2,1)S(1)}, u32[]{:S(2)}, u32[]{:S(2)}) async-start(bf16[16,16,256]{2,1,0:T(8,128)(2,1)} %broadcast_in_dim.6), calls=%async_computation.2 | async-start | bytes 262144 | tf_op jit(solution)/shard_map/all_to_all | solution.py:349
  81.5 0.0 copy-done.6
  81.6 0.1 pad.3.clone
  81.6 0.1 add_add_fusion
  81.7 0.1 reshape.78.index_ref
  81.8 3.0 %finish.1 = bf16[2048,256]{1,0:T(8,128)(2,1)} custom-call(s32[1,1280]{1,0:T(1,128)S(1)} %reshape.78.index_ref, f32[2048,256]{1,0:T(8,128)S(1)} %own.1.base_ref, bf16[1280,256]{1,0:T(8,128)(2,1)S(1)} %bitcast.13), custom_call_target="tpu_custom_call" | custom-call | tf_op jit(solution)/shard_map/finish/pallas_call | solution.py:419
  84.8 4.5 %all-to-all-done.2 = bf16[16,16,256]{2,1,0:T(8,128)(2,1)S(1)} async-done(((bf16[16,16,256]{2,1,0:T(8,128)(2,1)}), bf16[16,16,256]{2,1,0:T(8,128)(2,1)S(1)}, u32[]{:S(2)}, u32[]{:S(2)}) %all-to-all-start.2) | async-done | bytes 131104 | tf_op jit(solution)/shard_map/all_to_all | solution.py:349
  89.3 0.0 collective-permute-start.2
  89.3 1.3 %collective-permute-done.2 = bf16[256,256]{1,0:T(8,128)(2,1)S(1)} collective-permute-done((bf16[256,256]{1,0:T(8,128)(2,1)S(1)}, bf16[256,256]{1,0:T(8,128)(2,1)S(1)}, u32[]{:S(2)}, u32[]{:S(2)}) %collective-permute-start.2) | collective-permute-done | bytes 131104 | tf_op jit(solution)/shard_map/ppermute | solution.py:433
  90.6 0.8 select_convert_fusion
  (9 shorter events, 0.1 us)
Async XLA Ops:
  0.6 11.6 %copy-start.3 = (s32[65536]{0:T(1024)S(1)}, s32[65536]{0:T(1024)}, u32[]{:S(2)}) copy-start(s32[65536]{0:T(1024)} %param.15) | copy-start | bytes 786436
  0.6 11.6 %copy-start.4 = (s32[65536]{0:T(1024)S(1)}, s32[65536]{0:T(1024)}, u32[]{:S(2)}) copy-start(s32[65536]{0:T(1024)} %param.14) | copy-start | bytes 786436
  4.9 29.3 %all-to-all-start = ((bf16[32,48,256]{2,1,0:T(8,128)(2,1)}), bf16[32,48,256]{2,1,0:T(8,128)(2,1)S(1)}, u32[]{:S(2)}, u32[]{:S(2)}) async-start(bf16[32,48,256]{2,1,0:T(8,128)(2,1)} %bitcast.2), calls=%async_computation | async-start | bytes 1572864 | tf_op jit(solution)/shard_map/all_to_all | solution.py:233
  12.2 22.0 %copy-start = (bf16[2048,256]{1,0:T(8,128)(2,1)S(1)}, bf16[2048,256]{1,0:T(8,128)(2,1)}, u32[]{:S(2)}) copy-start(bf16[2048,256]{1,0:T(8,128)(2,1)} %feats_ref.3) | copy-start | bytes 3145732
  12.2 22.0 %copy-start.1 = (bf16[256,256]{1,0:T(8,128)(2,1)S(1)}, bf16[256,256]{1,0:T(8,128)(2,1)}, u32[]{:S(2)}) copy-start(bf16[256,256]{1,0:T(8,128)(2,1)} %ws_ref.3) | copy-start | bytes 393220
  12.2 22.0 %copy-start.2 = (bf16[256,256]{1,0:T(8,128)(2,1)S(1)}, bf16[256,256]{1,0:T(8,128)(2,1)}, u32[]{:S(2)}) copy-start(bf16[256,256]{1,0:T(8,128)(2,1)} %wn_ref.1) | copy-start | bytes 393220
  45.4 7.0 %collective-permute-start = (f32[256,256]{1,0:T(8,128)S(1)}, f32[256,256]{1,0:T(8,128)S(1)}, u32[]{:S(2)}, u32[]{:S(2)}) collective-permute-start(f32[256,256]{1,0:T(8,128)S(1)} %constant_dynamic-slice_fusion), channel_id=1, source_target_pairs={{0,8},{8,0},{16,24},{24,16},{1,9},{9,1},{17,25},{25,17},{2,10},{10... | collective-permute-start | bytes 786440 | tf_op jit(solution)/shard_map/ppermute | solution.py:372
  48.7 3.8 %collective-permute-start.1 = (bf16[768,256]{1,0:T(8,128)(2,1)S(1)}, bf16[768,256]{1,0:T(8,128)(2,1)S(1)}, u32[]{:S(2)}, u32[]{:S(2)}) collective-permute-start(bf16[768,256]{1,0:T(8,128)(2,1)S(1)} %far.2), channel_id=1, source_target_pairs={{0,8},{8,0},{16,24},{24,16},{1,9},{9,1},{17,25},{25,17},{2,10},{10... | collective-permute-start | bytes 1179656 | tf_op jit(solution)/shard_map/ppermute | solution.py:374
  52.6 6.6 %copy-start.5 = (s32[512]{0:T(512)S(1)}, s32[512]{0:T(512)}, u32[]{:S(2)}) copy-start(s32[512]{0:T(512)} %send_ref.1) | copy-start | bytes 6148
  53.5 23.8 %all-to-all-start.1 = ((bf16[16,80,256]{2,1,0:T(8,128)(2,1)}), bf16[16,80,256]{2,1,0:T(8,128)(2,1)S(1)}, u32[]{:S(2)}, u32[]{:S(2)}) async-start(bf16[16,80,256]{2,1,0:T(8,128)(2,1)} %pad_maximum_fusion), calls=%async_computation.1 | async-start | bytes 1310720 | tf_op jit(solution)/shard_map/all_to_all | solution.py:349
  59.3 22.2 %copy-start.6 = (s32[32]{0:T(128)S(1)}, s32[32]{0:T(128)}, u32[]{:S(2)}) copy-start(s32[32]{0:T(128)} %hub_ref.1) | copy-start | bytes 388
  78.0 11.3 %all-to-all-start.2 = ((bf16[16,16,256]{2,1,0:T(8,128)(2,1)}), bf16[16,16,256]{2,1,0:T(8,128)(2,1)S(1)}, u32[]{:S(2)}, u32[]{:S(2)}) async-start(bf16[16,16,256]{2,1,0:T(8,128)(2,1)} %broadcast_in_dim.6), calls=%async_computation.2 | async-start | bytes 262144 | tf_op jit(solution)/shard_map/all_to_all | solution.py:349
  89.3 1.3 %collective-permute-start.2 = (bf16[256,256]{1,0:T(8,128)(2,1)S(1)}, bf16[256,256]{1,0:T(8,128)(2,1)S(1)}, u32[]{:S(2)}, u32[]{:S(2)}) collective-permute-start(bf16[256,256]{1,0:T(8,128)(2,1)S(1)} %bitcast.20), channel_id=1, source_target_pairs={{0,8},{8,0},{16,24},{24,16},{1,9},{9,1},{17,25},{25,17},{2,10},{10... | collective-permute-start | bytes 393224 | tf_op jit(solution)/shard_map/ppermute | solution.py:433
